TPU v7x, 256 devices: a whole 4x4x8 slice. The times are simulated.
256 devices in a mesh: branch: 2 (over core), seq: 8 (over y, x_hi), rep: 16 (over z, x_lo).
Axes of the slice: x: 4 (x_hi: 2, x_lo: 2; x = x_hi * 2 + x_lo), y: 4, z: 8, core: 2. Of those that a mesh axis runs over, the one named last changes fastest.
Arguments:
- queries: bfloat16 [2, 16384, 2048], P('branch', ('rep', 'seq')), parts along dimension 1, may hold values from -64 to 64
- key_vecs: bfloat16 [2, 16384, 2048], P('branch', ('rep', 'seq')), parts along dimension 1, may hold values from -8 to 8
- value_vecs: bfloat16 [2, 16384, 2048], P('branch', ('rep', 'seq')), parts along dimension 1, may hold values from -6 to 6
- hidden_in: bfloat16 [2, 16384, 2048], P('branch', ('rep', 'seq')), parts along dimension 1, may hold values from -4 to 4
- out_proj: bfloat16 [2, 2048, 2048], P('branch', 'seq'), may hold values from -0.125 to 0.125
- couple_proj: bfloat16 [2, 2048, 2048], P('branch', 'seq'), may hold values from -0.125 to 0.125
- grad_mixed: bfloat16 [2, 16384, 2048], P('branch', ('rep', 'seq')), parts along dimension 1, may hold values from -6 to 6
Outputs:
- mixed_out: bfloat16 [2, 16384, 2048], P('branch', ('rep', 'seq')), parts along dimension 1
- grad_hidden: bfloat16 [2, 16384, 2048], P('branch', ('rep', 'seq')), parts along dimension 1
- grad_queries: bfloat16 [2, 16384, 2048], P('branch', ('rep', 'seq')), parts along dimension 1
- grad_keys: bfloat16 [2, 16384, 2048], P('branch', ('rep', 'seq')), parts along dimension 1
- grad_values: bfloat16 [2, 16384, 2048], P('branch', ('rep', 'seq')), parts along dimension 1
- grad_couple: float32 [2, 2048, 32768], P('branch', 'seq', 'rep'), parts along dimension 2
There are 16 independent parts, one for each index of `rep`. A program takes and returns all parts, laid end to end along the dimension named above; an argument that names none is the same for every part. Nothing has to cross between parts.
All inputs are finite; a program needn't handle non-finite values.
Results may differ from a plain program's by a relative error of at most 0.015.
Values may be sent and summed in bfloat16 or wider, within the bound.
No kernel may reach another device: no remote copies, remote signals or barrier semaphores. Data moves between devices by JAX's collectives and lax.ppermute only.
A program may use at most 128 MiB of HBM per device.

v0:
```python
import math

import jax
import jax.numpy as jnp
from jax import lax
from jax.experimental import pallas as pl
from jax.experimental.pallas import tpu as pltpu
from jax.sharding import PartitionSpec as P


HEAD = 128
TOK = 128
CHUNK = 256
WIDE = 2 * CHUNK
FACTOR = 1.0 / math.sqrt(HEAD)
BF16 = jnp.bfloat16
F32 = jnp.float32
VMEM_LIMIT = 56 * 1024 * 1024


def seq_shift(value, mask):
    size = lax.axis_size("seq")
    return lax.ppermute(value, "seq", [(i, i ^ mask) for i in range(size)])


def branch_swap(value):
    return lax.ppermute(value, "branch", [(0, 1), (1, 0)])


def partner_rows(weight):
    seqs, reps = lax.axis_size("seq"), lax.axis_size("rep")
    pairs = [
        (s * reps + r, (s ^ 1) * reps + (r ^ 1 if reps > 1 else r))
        for s in range(seqs)
        for r in range(reps)
    ]
    return lax.ppermute(weight, ("seq", "rep"), pairs)


def dot(left, right, left_dim, right_dim):
    return lax.dot_general(
        left, right, (((left_dim,), (right_dim,)), ((), ())), preferred_element_type=F32
    )


def full(shape):
    return pl.BlockSpec(shape, lambda *_: (0,) * len(shape))


def call(body, grid, in_specs, out_specs, out_shapes, seq, args, scratch=()):
    return pl.pallas_call(
        body,
        out_shape=out_shapes,
        grid_spec=pltpu.PrefetchScalarGridSpec(
            num_scalar_prefetch=1,
            grid=grid,
            in_specs=in_specs,
            out_specs=out_specs,
            scratch_shapes=list(scratch),
        ),
        compiler_params=pltpu.CompilerParams(
            vmem_limit_bytes=VMEM_LIMIT, dimension_semantics=("arbitrary",) * len(grid)
        ),
    )(seq, *args)


def chunk_spec(rows, rel):
    return pl.BlockSpec((rows, CHUNK), lambda i, seq: (0, seq[0] ^ rel))


def sds(shape, dtype=BF16):
    return jax.ShapeDtypeStruct(shape, dtype)


def relative_columns(seq, arrays):
    count = len(arrays)

    def body(seq_ref, *refs):
        ins, outs = refs[: 8 * count], refs[8 * count :]
        for a in range(count):
            for rel in range(8):
                half = rel & 1
                outs[rel >> 1][a, :, half * CHUNK : (half + 1) * CHUNK] = ins[8 * a + rel][...]

    in_specs = [chunk_spec(TOK, rel) for _ in arrays for rel in range(8)]
    args = [array for array in arrays for _ in range(8)]
    return call(
        body,
        (1,),
        in_specs,
        [full((count, TOK, WIDE))] * 4,
        [sds((count, TOK, WIDE))] * 4,
        seq,
        args,
    )


def absolute_columns(seq, halves):
    flat = [block for piece in halves for pair in piece for block in pair]
    count = len(halves[0])

    def body(seq_ref, *refs):
        ins, outs = refs[: 8 * count], refs[8 * count :]
        step = pl.program_id(0)
        odd = (seq_ref[0] & 1) == 1
        for rel in range(4):

            @pl.when(step == rel)
            def _(rel=rel):
                for a in range(count):
                    low = ins[2 * (rel * count + a)][...]
                    high = ins[2 * (rel * count + a) + 1][...]
                    outs[a][:, :CHUNK] = jnp.where(odd, high, low)
                    outs[a][:, CHUNK:] = jnp.where(odd, low, high)

    out_spec = pl.BlockSpec((TOK, WIDE), lambda i, seq: (0, (seq[0] >> 1) ^ i))
    return call(
        body,
        (4,),
        [spec for _, spec in flat],
        [out_spec] * count,
        [sds((TOK, 8 * CHUNK))] * count,
        seq,
        [array for array, _ in flat],
    )


def back_couple_product(seq, grads, couple):
    def body(seq_ref, g0, g1, g2, g3, w0, w1, out):
        rows = jnp.concatenate([g0[...], g1[...], g2[...], g3[...]], axis=0)
        out[:, :CHUNK] = dot(rows, w0[...], 1, 1).astype(BF16)
        out[:, CHUNK:] = dot(rows, w1[...], 1, 1).astype(BF16)

    specs = [full((TOK, 8 * CHUNK))] * 4 + [full((CHUNK, 8 * CHUNK))] * 2
    return call(
        body,
        (1,),
        specs,
        full((4 * TOK, WIDE)),
        sds((4 * TOK, WIDE)),
        seq,
        (*grads, *couple),
    )


def grad_hidden_chunk(seq, grads, partner_back):
    def body(seq_ref, *refs):
        ins, back, out = refs[:8], refs[8], refs[9]
        for r in range(4):
            for h in range(2):
                rows = slice(r * TOK, (r + 1) * TOK)
                cols = slice(h * CHUNK, (h + 1) * CHUNK)
                total = ins[2 * r + h][...].astype(F32) + back[rows, cols].astype(F32)
                out[rows, cols] = total.astype(BF16)

    specs = [chunk_spec(TOK, h) for _ in range(4) for h in range(2)]
    args = [grad for grad in grads for _ in range(2)]
    return call(
        body,
        (1,),
        specs + [full((4 * TOK, WIDE))],
        full((4 * TOK, WIDE)),
        sds((4 * TOK, WIDE)),
        seq,
        (*args, partner_back),
    )


def proj_specs():
    return [chunk_spec(CHUNK, rel) for _ in range(2) for rel in range(8)]


def head_specs(first):
    query = pl.BlockSpec((None, TOK, HEAD), lambda j, seq: (0, 0, j + first))
    pair = pl.BlockSpec((2, TOK, HEAD), lambda j, seq: (0, 0, j + first))
    other = pl.BlockSpec((2, TOK, HEAD), lambda j, seq: (0, 0, (j + first + 2) % 4))
    return [query] * 4 + [pair] * 4 + [other] * 4


def head_values(refs):
    query = jnp.concatenate([ref[...] for ref in refs[:4]], axis=0)
    key = jnp.concatenate([ref[0] for ref in refs[4:12]], axis=0)
    value = jnp.concatenate([ref[1] for ref in refs[4:12]], axis=0)
    return query, key, value


def raised_scores(query, key):
    scores = dot(query, key, 1, 1)
    base = FACTOR * math.log2(math.e)
    return jnp.exp2(scores * base - jnp.max(scores, axis=-1, keepdims=True) * base)


def attend(seq, heads):
    def body(seq_ref, *refs):
        query, key, value = head_values(refs)
        raised = raised_scores(query, key)
        total = jnp.sum(raised, axis=-1, keepdims=True)
        refs[12][...] = (dot(raised.astype(BF16), value, 1, 0) / total).astype(BF16)

    return call(
        body,
        (4,),
        head_specs(0),
        pl.BlockSpec((4 * TOK, HEAD), lambda j, seq: (0, j)),
        sds((4 * TOK, WIDE)),
        seq,
        heads,
    )


def output_partial(seq, attended, proj):
    def body(seq_ref, att, *refs):
        weights, outs = refs[:16], refs[16:]
        first, second = att[:, :CHUNK], att[:, CHUNK:]
        for rel in range(8):
            dest, half = rel >> 1, rel & 1
            part = dot(first, weights[rel][...], 1, 0) + dot(second, weights[8 + rel][...], 1, 0)
            for r in range(4):
                rows = (r ^ dest) * TOK
                outs[dest][rows : rows + TOK, half * CHUNK : (half + 1) * CHUNK] = part[
                    r * TOK : (r + 1) * TOK
                ].astype(outs[dest].dtype)

    return call(
        body,
        (1,),
        [full((4 * TOK, WIDE))] + proj_specs(),
        [full((4 * TOK, WIDE))] * 4,
        [sds((4 * TOK, WIDE), F32)] + [sds((4 * TOK, WIDE))] * 3,
        seq,
        (attended, *([proj[0]] * 8), *([proj[1]] * 8)),
    )


def hidden_sum(seq, items, own, received):
    def body(seq_ref, i0, i1, i2, i3, own_ref, r1, r2, r3, out):
        for r, item in enumerate((i0, i1, i2, i3)):
            rows = slice(r * TOK, (r + 1) * TOK)
            total = item[...].astype(F32) + own_ref[rows]
            total = total + r1[rows].astype(F32) + r2[rows].astype(F32) + r3[rows].astype(F32)
            out[rows] = total.astype(BF16)

    item_spec = pl.BlockSpec((None, TOK, WIDE), lambda i, seq: (0, 0, 0))
    return call(
        body,
        (1,),
        [item_spec] * 4 + [full((4 * TOK, WIDE))] * 4,
        full((4 * TOK, WIDE)),
        sds((4 * TOK, WIDE)),
        seq,
        (*items, own, *received),
    )


def mixed_partial(seq, partner_hidden, hidden, couple):
    def body(seq_ref, ph, hid, w0, w1, o0, o1, o2, o3):
        part = dot(ph[:, :CHUNK], w0[...], 1, 0) + dot(ph[:, CHUNK:], w1[...], 1, 0)
        first = pl.program_id(0) == 0
        odd = (seq_ref[0] & 1) == 1
        outs = (o0, o1, o2, o3)

        @pl.when(first)
        def _():
            low = hid[:, :CHUNK].astype(F32)
            high = hid[:, CHUNK:].astype(F32)
            own = jnp.concatenate([jnp.where(odd, high, low), jnp.where(odd, low, high)], axis=1)
            for r in range(4):
                rows = slice(r * TOK, (r + 1) * TOK)
                outs[r][...] = (part[rows] + own[rows]).astype(outs[r].dtype)

        @pl.when(jnp.logical_not(first))
        def _():
            for r in range(4):
                rows = slice(r * TOK, (r + 1) * TOK)
                outs[r][...] = part[rows].astype(outs[r].dtype)

    wide_cols = lambda rows: pl.BlockSpec((rows, WIDE), lambda i, seq: (0, (seq[0] >> 1) ^ i))
    return call(
        body,
        (4,),
        [full((4 * TOK, WIDE))] * 2 + [wide_cols(CHUNK)] * 2,
        [wide_cols(TOK)] * 4,
        [sds((TOK, 8 * CHUNK), F32)] + [sds((TOK, 8 * CHUNK))] * 3,
        seq,
        (partner_hidden, hidden, *couple),
    )


def couple_gradient(seq, partner_hidden, grads):
    def body(seq_ref, ph, g0, g1, g2, g3, own, other):
        rows = jnp.concatenate([g0[...], g1[...], g2[...], g3[...]], axis=0)
        other[...] = dot(ph[:, CHUNK:], rows, 0, 0).astype(BF16)
        own[...] = dot(ph[:, :CHUNK], rows, 0, 0)

    cols = lambda rows: pl.BlockSpec((rows, WIDE), lambda i, seq: (0, i))
    return call(
        body,
        (4,),
        [full((4 * TOK, WIDE))] + [cols(TOK)] * 4,
        [cols(CHUNK)] * 2,
        [sds((CHUNK, 8 * CHUNK), F32), sds((CHUNK, 8 * CHUNK))],
        seq,
        (partner_hidden, *grads),
    )


def backward_half(seq, heads, grad_chunks, proj_rows, half):
    def body(seq_ref, *refs):
        chunks, weights = refs[12:16], refs[16:24]
        dq_out, kv_own, kv_other, grad_att = refs[24:28]
        step = pl.program_id(0)

        @pl.when(step == 0)
        def _():
            total = None
            for d, chunk in enumerate(chunks):
                rows = jnp.concatenate(
                    [chunk[(r ^ d) * TOK : ((r ^ d) + 1) * TOK] for r in range(4)], axis=0
                )
                for h in range(2):
                    piece = rows[:, h * CHUNK : (h + 1) * CHUNK]
                    term = dot(piece, weights[2 * d + h][...], 1, 1)
                    total = term if total is None else total + term
            grad_att[0] = total[:, :HEAD].astype(BF16)
            grad_att[1] = total[:, HEAD:].astype(BF16)

        grad = grad_att[step]
        query, key, value = head_values(refs)
        raised = raised_scores(query, key)
        weight = raised * (1.0 / jnp.sum(raised, axis=-1, keepdims=True))
        grad_weight = dot(grad, value, 1, 1)
        row_dot = jnp.sum(weight * grad_weight, axis=-1, keepdims=True)
        d_scores = (weight * (grad_weight - row_dot)).astype(BF16)
        dq_out[...] = (dot(d_scores, key, 1, 0) * FACTOR).astype(BF16)
        d_key = (dot(d_scores, query, 0, 0) * FACTOR).astype(BF16)
        d_value = dot(weight.astype(BF16), grad, 0, 0).astype(BF16)
        rows = 4 * TOK
        kv_own[0] = d_key[:rows]
        kv_own[1] = d_value[:rows]
        kv_other[0] = d_key[rows:]
        kv_other[1] = d_value[rows:]

    pair = pl.BlockSpec((2, 4 * TOK, HEAD), lambda j, seq: (0, 0, j))
    return call(
        body,
        (2,),
        head_specs(2 * half)
        + [full((4 * TOK, WIDE))] * 4
        + [chunk_spec(CHUNK, rel) for rel in range(8)],
        [pl.BlockSpec((4 * TOK, HEAD), lambda j, seq: (0, j)), pair, pair],
        [sds((4 * TOK, CHUNK))] + [sds((2, 4 * TOK, CHUNK))] * 2,
        seq,
        (*heads, *grad_chunks, *([proj_rows] * 8)),
        scratch=[pltpu.VMEM((2, 4 * TOK, HEAD), BF16)],
    )


def add_key_grads(seq, own, other, query_grads):
    count = 2 + len(query_grads)

    def body(seq_ref, a, b, *refs):
        ins, outs = refs[: count - 2], refs[count - 2 :]
        for r, out in enumerate(outs):
            rows = slice(r * TOK, (r + 1) * TOK)
            for t in range(2):
                out[t] = (a[t, rows].astype(F32) + b[t, rows].astype(F32)).astype(BF16)
            for t, ref in enumerate(ins):
                out[2 + t] = ref[rows]

    return call(
        body,
        (1,),
        [full((2, 4 * TOK, CHUNK))] * 2 + [full((4 * TOK, CHUNK))] * (count - 2),
        [full((count, TOK, CHUNK))] * 4,
        [sds((count, TOK, CHUNK))] * 4,
        seq,
        (own, other, *query_grads),
    )


def exchange(pieces):
    got = [pieces[0], None, None, None]
    for r in (2, 1, 3):
        got[r] = seq_shift(pieces[r], 2 * r)
    return got


def half_block(array, lead):
    return (array, pl.BlockSpec((None, TOK, CHUNK), lambda i, seq: (lead, 0, 0)))


def steps(queries, key_vecs, value_vecs, hidden_in, out_proj, couple_proj, grad_mixed):
    seq = lax.axis_index("seq").astype(jnp.int32).reshape(1)
    pairs = relative_columns(seq, (key_vecs[0], value_vecs[0]))
    pairs = exchange(pairs)
    others = [seq_shift(pairs[r], 1) for r in range(4)]
    items = exchange(relative_columns(seq, (queries[0],)))
    grads = exchange([grad_mixed[0]] * 4)
    couple = (couple_proj[0], partner_rows(couple_proj[0]))
    inputs = exchange(relative_columns(seq, (hidden_in[0],)))
    late_proj, _ = lax.optimization_barrier((out_proj[0], couple[1]))
    proj = (out_proj[0], partner_rows(late_proj))
    heads = (*items, *pairs, *others)

    back = back_couple_product(seq, grads, couple)
    partner_back = branch_swap(back)
    chunk = grad_hidden_chunk(seq, grads, partner_back)
    chunks = exchange([chunk] * 4)

    sums = exchange(output_partial(seq, attend(seq, heads), proj))

    first = backward_half(seq, heads, chunks, proj[0], 0)
    got_high = seq_shift(first[2], 1)
    second = backward_half(seq, heads, chunks, proj[1], 1)
    got_low = seq_shift(second[2], 1)

    hidden = hidden_sum(seq, inputs, sums[0], sums[1:])
    partner_hidden = branch_swap(hidden)
    mixed_parts = exchange(mixed_partial(seq, partner_hidden, hidden, couple))
    couple_own, couple_other = couple_gradient(seq, partner_hidden, grads)
    couple_got = seq_shift(couple_other, 1)

    high = add_key_grads(seq, second[1], got_high, (first[0], second[0]))
    high = exchange(high)
    low = exchange(add_key_grads(seq, first[1], got_low, ()))

    def chunk_half(r, h):
        return (chunks[r], pl.BlockSpec((TOK, CHUNK), lambda i, seq: (r, h)))

    (grad_hid,) = absolute_columns(
        seq, [[(chunk_half(r, 0), chunk_half(r, 1))] for r in range(4)]
    )
    mixed = mixed_parts[0]
    for part in mixed_parts[1:]:
        mixed = mixed + part.astype(F32)
    grad_cpl = couple_own + couple_got.astype(F32)
    grad_q, grad_k, grad_v = absolute_columns(
        seq,
        [
            [
                (half_block(high[r], 2), half_block(high[r], 3)),
                (half_block(low[r], 0), half_block(high[r], 0)),
                (half_block(low[r], 1), half_block(high[r], 1)),
            ]
            for r in range(4)
        ],
    )
    return (
        mixed.astype(BF16)[None],
        grad_hid[None],
        grad_q[None],
        grad_k[None],
        grad_v[None],
        grad_cpl[None],
    )


def solution(mesh):
    return jax.shard_map(
        steps,
        mesh=mesh,
        in_specs=(
            P("branch", ("rep", "seq"), None),
            P("branch", ("rep", "seq"), None),
            P("branch", ("rep", "seq"), None),
            P("branch", ("rep", "seq"), None),
            P("branch", "seq", None),
            P("branch", "seq", None),
            P("branch", ("rep", "seq"), None),
        ),
        out_specs=(
            P("branch", ("rep", "seq"), None),
            P("branch", ("rep", "seq"), None),
            P("branch", ("rep", "seq"), None),
            P("branch", ("rep", "seq"), None),
            P("branch", ("rep", "seq"), None),
            P("branch", "seq", "rep"),
        ),
        check_vma=False,
    )
```

profile of v0, /device:TPU:1, one launch (start us, length us, event | category | flops | bytes accessed | tf_op | source)
XLA Modules:
  0.0 205.7 jit_solution(10418742321874488057)
XLA Ops:
  0.6 3.4 %collective-permute-start.13 = (bf16[256,2048]{1,0:T(8,128)(2,1)}, bf16[256,2048]{1,0:T(8,128)(2,1)S(1)}, u32[]{:S(2)}, u32[]{:S(2)}) collective-permute-start(bf16[256,2048]{1,0:T(8,128)(2,1)} %bitcast.72), channel_id=1, source_target_pairs={{0,17},{1,16},{2,19},{3,18},{4,21},{5,20},{6,23},{7,22},{8,25},{9,... | collective-permute-start | bytes 3145736 | tf_op jit(solution)/shard_map/ppermute | solution.py:37
  5.3 2.6 %collective-permute-start.23 = (bf16[128,2048]{1,0:T(8,128)(2,1)}, bf16[128,2048]{1,0:T(8,128)(2,1)S(1)}, u32[]{:S(2)}, u32[]{:S(2)}) collective-permute-start(bf16[128,2048]{1,0:T(8,128)(2,1)} %bitcast.66), channel_id=1, source_target_pairs={{0,64},{16,80},{32,96},{48,112},{64,0},{80,16},{96,32},{112,48},{1... | collective-permute-start | bytes 1572872 | tf_op jit(solution)/shard_map/ppermute | solution.py:23
  7.9 8.8 %collective-permute-done.22.g1.refs_2_.refs_3_ = bf16[128,2048]{1,0:T(8,128)(2,1)S(1)} collective-permute-done((bf16[128,2048]{1,0:T(8,128)(2,1)}, bf16[128,2048]{1,0:T(8,128)(2,1)S(1)}, u32[]{:S(2)}, u32[]{:S(2)}) %collective-permute-start.22) | collective-permute-done | bytes 524320 | tf_op jit(solution)/shard_map/ppermute | solution.py:23
  16.8 13.7 %collective-permute-done.23.g2.refs_4_.refs_5_ = bf16[128,2048]{1,0:T(8,128)(2,1)S(1)} collective-permute-done((bf16[128,2048]{1,0:T(8,128)(2,1)}, bf16[128,2048]{1,0:T(8,128)(2,1)S(1)}, u32[]{:S(2)}, u32[]{:S(2)}) %collective-permute-start.23) | collective-permute-done | bytes 524320 | tf_op jit(solution)/shard_map/ppermute | solution.py:23
  30.5 2.1 %collective-permute-done.24.g3.refs_6_.refs_7_ = bf16[128,2048]{1,0:T(8,128)(2,1)S(1)} collective-permute-done((bf16[128,2048]{1,0:T(8,128)(2,1)}, bf16[128,2048]{1,0:T(8,128)(2,1)S(1)}, u32[]{:S(2)}, u32[]{:S(2)}) %collective-permute-start.24) | collective-permute-done | bytes 524320 | tf_op jit(solution)/shard_map/ppermute | solution.py:23
  33.7 4.3 %shard_map.125 = bf16[512,512]{1,0:T(8,128)(2,1)} custom-call(s32[1]{0:T(128)} %bitcast.seq_ref, bf16[128,2048]{1,0:T(8,128)(2,1)} %bitcast.68, bf16[128,2048]{1,0:T(8,128)(2,1)} %copy-done.5, bf16[128,2048]{1,0:T(8,128)(2,1)} %copy-done.6, bf16[128,2048]{1,0:T(8,128)(2,1)} %copy-done.7, bf16[256,2048]{1,0:T(8,128)(2,1)} %bitcast.73, bf16[256,2048]{1,0:T(8,128)(2,1)} %copy-done.8), custom_call_target="tpu_custom_call" | custom-call | tf_op jit(solution)/shard_map/pallas_call | solution.py:51
  38.1 2.4 %collective-permute-start.25 = (bf16[512,512]{1,0:T(8,128)(2,1)}, bf16[512,512]{1,0:T(8,128)(2,1)S(1)}, u32[]{:S(2)}, u32[]{:S(2)}) collective-permute-start(bf16[512,512]{1,0:T(8,128)(2,1)} %shard_map.125), channel_id=1, source_target_pairs={{0,128},{128,0},{1,129},{129,1},{2,130},{130,2},{3,131},{131,3},{4... | collective-permute-start | bytes 1572872 | tf_op jit(solution)/shard_map/ppermute | solution.py:27
  42.5 2.3 %shard_map.120 = (bf16[2,128,512]{2,1,0:T(8,128)(2,1)}, bf16[2,128,512]{2,1,0:T(8,128)(2,1)}, bf16[2,128,512]{2,1,0:T(8,128)(2,1)}, bf16[2,128,512]{2,1,0:T(8,128)(2,1)}) custom-call(s32[1]{0:T(128)} %bitcast.seq_ref, bf16[128,2048]{1,0:T(8,128)(2,1)} %bitcast.41, bf16[128,2048]{1,0:T(8,128)(2,1)} %bitcast.42, bf16[128,2048]{1,0:T(8,128)(2,1)} %bitcast.43, ...), custom_call_target="tpu_custom_call" | custom-call | tf_op jit(solution)/shard_map/pallas_call | solution.py:51
  48.8 7.2 %collective-permute-done.4.refs_2_ = bf16[1,128,512]{2,1,0:T(8,128)(2,1)S(1)} collective-permute-done((bf16[1,128,512]{2,1,0:T(8,128)(2,1)S(1)}, bf16[1,128,512]{2,1,0:T(8,128)(2,1)S(1)}, u32[]{:S(2)}, u32[]{:S(2)}) %collective-permute-start.4) | collective-permute-done | bytes 131104 | tf_op jit(solution)/shard_map/ppermute | solution.py:23
  56.0 2.0 collective-permute-start.7
  61.7 2.2 %shard_map.126.refs_0_.refs_1_.refs_12_ = bf16[512,512]{1,0:T(8,128)(2,1)} custom-call(s32[1]{0:T(128)} %bitcast.seq_ref, bf16[128,2048]{1,0:T(8,128)(2,1)} %bitcast.69, bf16[128,2048]{1,0:T(8,128)(2,1)} %bitcast.70, bf16[128,2048]{1,0:T(8,128)(2,1)} %copy-done.5, bf16[128,2048]{1,0:T(8,128)(2,1)} %copy-done.5, bf16[128,2048]{1,0:T(8,128)(2,1)} %copy-done.6, ...), custom_call_target="tpu_custom_call" | custom-call | tf_op jit(solution)/shard_map/pallas_call | solution.py:51
  64.9 6.7 %collective-permute-done.8.refs_7_ = bf16[2,128,512]{2,1,0:T(8,128)(2,1)S(1)} collective-permute-done((bf16[2,128,512]{2,1,0:T(8,128)(2,1)}, bf16[2,128,512]{2,1,0:T(8,128)(2,1)S(1)}, u32[]{:S(2)}, u32[]{:S(2)}) %collective-permute-start.8) | collective-permute-done | bytes 262176 | tf_op jit(solution)/shard_map/ppermute | solution.py:23
  74.6 2.0 collective-permute-start.27
  76.5 4.0 %collective-permute-done.11.refs_10_ = bf16[2,128,512]{2,1,0:T(8,128)(2,1)S(1)} collective-permute-done((bf16[2,128,512]{2,1,0:T(8,128)(2,1)S(1)}, bf16[2,128,512]{2,1,0:T(8,128)(2,1)S(1)}, u32[]{:S(2)}, u32[]{:S(2)}) %collective-permute-start.11) | collective-permute-done | bytes 262176 | tf_op jit(solution)/shard_map/ppermute | solution.py:23
  80.5 2.1 %collective-permute-start.28 = (bf16[512,512]{1,0:T(8,128)(2,1)}, bf16[512,512]{1,0:T(8,128)(2,1)S(1)}, u32[]{:S(2)}, u32[]{:S(2)}) collective-permute-start(bf16[512,512]{1,0:T(8,128)(2,1)} %shard_map.126.refs_0_.refs_1_.refs_12_), channel_id=1, source_target_pairs={{0,96},{16,112},{32,64},{48,80},{64,32},{80,48},{96,0},{112,16},{1... | collective-permute-start | bytes 1572872 | tf_op jit(solution)/shard_map/ppermute | solution.py:23
  86.8 8.1 %shard_map.121.att = bf16[512,512]{1,0:T(8,128)(2,1)} custom-call(s32[1]{0:T(128)} %bitcast.seq_ref, bf16[1,128,512]{2,1,0:T(8,128)(2,1)} %get-tuple-element.50.refs_0_, bf16[1,128,512]{2,1,0:T(8,128)(2,1)} %copy-done.21, bf16[1,128,512]{2,1,0:T(8,128)(2,1)} %copy-done.22, bf16[1,128,512]{2,1,0:T(8,128)(2,1)} %copy-done.23, ...), custom_call_target="tpu_custom_call" | custom-call | tf_op jit(solution)/shard_map/pallas_call | solution.py:51
  95.9 3.8 %shard_map.122 = (f32[512,512]{1,0:T(8,128)}, bf16[512,512]{1,0:T(8,128)(2,1)}, bf16[512,512]{1,0:T(8,128)(2,1)}, bf16[512,512]{1,0:T(8,128)(2,1)}) custom-call(s32[1]{0:T(128)} %bitcast.seq_ref, bf16[512,512]{1,0:T(8,128)(2,1)} %shard_map.121.att, bf16[256,2048]{1,0:T(8,128)(2,1)} %bitcast.16, bf16[256,2048]{1,0:T(8,128)(2,1)} %bitcast.17, ...), custom_call_target="tpu_custom_call" | custom-call | tf_op jit(solution)/shard_map/pallas_call | solution.py:51
  100.5 2.5 %collective-permute-start.16 = (bf16[512,512]{1,0:T(8,128)(2,1)}, bf16[512,512]{1,0:T(8,128)(2,1)S(1)}, u32[]{:S(2)}, u32[]{:S(2)}) collective-permute-start(bf16[512,512]{1,0:T(8,128)(2,1)} %get-tuple-element.61), channel_id=1, source_target_pairs={{0,64},{16,80},{32,96},{48,112},{64,0},{80,16},{96,32},{112,48},{1... | collective-permute-start | bytes 1572872 | tf_op jit(solution)/shard_map/ppermute | solution.py:23
  105.9 8.3 %shard_map.129 = (bf16[512,256]{1,0:T(8,128)(2,1)}, bf16[2,512,256]{2,1,0:T(8,128)(2,1)}, bf16[2,512,256]{2,1,0:T(8,128)(2,1)}) custom-call(s32[1]{0:T(128)} %bitcast.seq_ref, bf16[1,128,512]{2,1,0:T(8,128)(2,1)} %get-tuple-element.50.refs_0_, bf16[1,128,512]{2,1,0:T(8,128)(2,1)} %copy-done.21, bf16[1,128,512]{2,1,0:T(8,128)(2,1)} %copy-done.22, ...), custom_call_target="tpu_custom_call" | custom-call | tf_op jit(solution)/shard_map/pallas_call | solution.py:51
  114.3 13.5 %collective-permute-done.1.i2 = bf16[1,128,512]{2,1,0:T(8,128)(2,1)S(1)} collective-permute-done((bf16[1,128,512]{2,1,0:T(8,128)(2,1)S(1)}, bf16[1,128,512]{2,1,0:T(8,128)(2,1)S(1)}, u32[]{:S(2)}, u32[]{:S(2)}) %collective-permute-start.1) | collective-permute-done | bytes 131104 | tf_op jit(solution)/shard_map/ppermute | solution.py:23
  129.2 8.2 %shard_map.128 = (bf16[512,256]{1,0:T(8,128)(2,1)}, bf16[2,512,256]{2,1,0:T(8,128)(2,1)}, bf16[2,512,256]{2,1,0:T(8,128)(2,1)}) custom-call(s32[1]{0:T(128)} %bitcast.seq_ref, bf16[1,128,512]{2,1,0:T(8,128)(2,1)} %get-tuple-element.50.refs_0_, bf16[1,128,512]{2,1,0:T(8,128)(2,1)} %copy-done.21, bf16[1,128,512]{2,1,0:T(8,128)(2,1)} %copy-done.22, ...), custom_call_target="tpu_custom_call" | custom-call | tf_op jit(solution)/shard_map/pallas_call | solution.py:51
  140.5 3.0 %shard_map.123.hid = bf16[512,512]{1,0:T(8,128)(2,1)} custom-call(s32[1]{0:T(128)} %bitcast.seq_ref, bf16[1,128,512]{2,1,0:T(8,128)(2,1)} %get-tuple-element.46.i0, bf16[1,128,512]{2,1,0:T(8,128)(2,1)} %copy-done.34, bf16[1,128,512]{2,1,0:T(8,128)(2,1)} %copy-done.35, bf16[1,128,512]{2,1,0:T(8,128)(2,1)} %copy-done.36, ...), custom_call_target="tpu_custom_call" | custom-call | tf_op jit(solution)/shard_map/pallas_call | solution.py:51
  143.5 3.0 %collective-permute-start.18 = (bf16[512,512]{1,0:T(8,128)(2,1)}, bf16[512,512]{1,0:T(8,128)(2,1)S(1)}, u32[]{:S(2)}, u32[]{:S(2)}) collective-permute-start(bf16[512,512]{1,0:T(8,128)(2,1)} %shard_map.123.hid), channel_id=1, source_target_pairs={{0,128},{128,0},{1,129},{129,1},{2,130},{130,2},{3,131},{131,3},{4... | collective-permute-start | bytes 1572872 | tf_op jit(solution)/shard_map/ppermute | solution.py:27
  147.3 2.4 %shard_map.130 = (bf16[4,128,256]{2,1,0:T(8,128)(2,1)}, bf16[4,128,256]{2,1,0:T(8,128)(2,1)}, bf16[4,128,256]{2,1,0:T(8,128)(2,1)}, bf16[4,128,256]{2,1,0:T(8,128)(2,1)}) custom-call(s32[1]{0:T(128)} %bitcast.seq_ref, bf16[2,512,256]{2,1,0:T(8,128)(2,1)} %get-tuple-element.67.a, bf16[2,512,256]{2,1,0:T(8,128)(2,1)} %copy-done.28, ...), custom_call_target="tpu_custom_call" | custom-call | tf_op jit(solution)/shard_map/pallas_call | solution.py:51
  149.8 2.9 %collective-permute-done.30.b = bf16[2,512,256]{2,1,0:T(8,128)(2,1)S(1)} collective-permute-done((bf16[2,512,256]{2,1,0:T(8,128)(2,1)}, bf16[2,512,256]{2,1,0:T(8,128)(2,1)S(1)}, u32[]{:S(2)}, u32[]{:S(2)}) %collective-permute-start.30) | collective-permute-done | bytes 524320 | tf_op jit(solution)/shard_map/ppermute | solution.py:23
  153.5 2.0 shard_map.131
  155.5 2.0 collective-permute-start.34
  160.2 5.2 %shard_map.124 = (f32[128,2048]{1,0:T(8,128)}, bf16[128,2048]{1,0:T(8,128)(2,1)}, bf16[128,2048]{1,0:T(8,128)(2,1)}, bf16[128,2048]{1,0:T(8,128)(2,1)}) custom-call(s32[1]{0:T(128)} %bitcast.seq_ref, bf16[512,512]{1,0:T(8,128)(2,1)} %copy-done.20, bf16[512,512]{1,0:T(8,128)(2,1)} %shard_map.123.hid, bf16[256,2048]{1,0:T(8,128)(2,1)} %bitcast.74, ...), custom_call_target="tpu_custom_call" | custom-call | tf_op jit(solution)/shard_map/pallas_call | solution.py:51
  168.7 5.1 %shard_map.133 = (f32[256,2048]{1,0:T(8,128)}, bf16[256,2048]{1,0:T(8,128)(2,1)}) custom-call(s32[1]{0:T(128)} %bitcast.seq_ref, bf16[512,512]{1,0:T(8,128)(2,1)} %copy-done.20, bf16[128,2048]{1,0:T(8,128)(2,1)} %bitcast.71, bf16[128,2048]{1,0:T(8,128)(2,1)} %copy-done.5, bf16[128,2048]{1,0:T(8,128)(2,1)} %copy-done.6, bf16[128,2048]{1,0:T(8,128)(2,1)} %copy-done.7), custom_call_target="tpu_custom_call" | custom-call | tf_op jit(solution)/shard_map/pallas_call | solution.py:51
  176.5 2.5 %shard_map.127 = bf16[128,2048]{1,0:T(8,128)(2,1)} custom-call(s32[1]{0:T(128)} %bitcast.seq_ref, bf16[512,512]{1,0:T(8,128)(2,1)} %shard_map.126.refs_0_.refs_1_.refs_12_, bf16[512,512]{1,0:T(8,128)(2,1)} %shard_map.126.refs_0_.refs_1_.refs_12_, bf16[512,512]{1,0:T(8,128)(2,1)} %copy-done.2, bf16[512,512]{1,0:T(8,128)(2,1)} %copy-done.2, ...), custom_call_target="tpu_custom_call" | custom-call | tf_op jit(solution)/shard_map/pallas_call | solution.py:51
  179.0 19.3 %collective-permute-done.35.refs_18_.refs_19_.refs_21_.refs_23_ = bf16[4,128,256]{2,1,0:T(8,128)(2,1)S(1)} collective-permute-done((bf16[4,128,256]{2,1,0:T(8,128)(2,1)S(1)}, bf16[4,128,256]{2,1,0:T(8,128)(2,1)S(1)}, u32[]{:S(2)}, u32[]{:S(2)}) %collective-permute-start.35) | collective-permute-done | bytes 262176 | tf_op jit(solution)/shard_map/ppermute | solution.py:23
  199.1 3.3 %shard_map.132 = (bf16[128,2048]{1,0:T(8,128)(2,1)}, bf16[128,2048]{1,0:T(8,128)(2,1)}, bf16[128,2048]{1,0:T(8,128)(2,1)}) custom-call(s32[1]{0:T(128)} %bitcast.seq_ref, bf16[4,128,256]{2,1,0:T(8,128)(2,1)} %get-tuple-element.71.refs_0_.refs_1_.refs_3_.refs_5_, bf16[4,128,256]{2,1,0:T(8,128)(2,1)} %get-tuple-element.71.refs_0_.refs_1_.refs_3_.refs_5_, ...), custom_call_target="tpu_custom_call" | custom-call | tf_op jit(solution)/shard_map/pallas_call | solution.py:51
  (146 shorter events, 43.9 us)
Async XLA Ops:
  0.6 31.9 %collective-permute-start.13 = (bf16[256,2048]{1,0:T(8,128)(2,1)}, bf16[256,2048]{1,0:T(8,128)(2,1)S(1)}, u32[]{:S(2)}, u32[]{:S(2)}) collective-permute-start(bf16[256,2048]{1,0:T(8,128)(2,1)} %bitcast.72), channel_id=1, source_target_pairs={{0,17},{1,16},{2,19},{3,18},{4,21},{5,20},{6,23},{7,22},{8,25},{9,... | collective-permute-start | bytes 3145736 | tf_op jit(solution)/shard_map/ppermute | solution.py:37
  4.0 12.7 %collective-permute-start.22 = (bf16[128,2048]{1,0:T(8,128)(2,1)}, bf16[128,2048]{1,0:T(8,128)(2,1)S(1)}, u32[]{:S(2)}, u32[]{:S(2)}) collective-permute-start(bf16[128,2048]{1,0:T(8,128)(2,1)} %bitcast.65), channel_id=1, source_target_pairs={{0,32},{16,48},{32,0},{48,16},{64,96},{80,112},{96,64},{112,80},{1... | collective-permute-start | bytes 1572872 | tf_op jit(solution)/shard_map/ppermute | solution.py:23
  5.3 25.2 %collective-permute-start.23 = (bf16[128,2048]{1,0:T(8,128)(2,1)}, bf16[128,2048]{1,0:T(8,128)(2,1)S(1)}, u32[]{:S(2)}, u32[]{:S(2)}) collective-permute-start(bf16[128,2048]{1,0:T(8,128)(2,1)} %bitcast.66), channel_id=1, source_target_pairs={{0,64},{16,80},{32,96},{48,112},{64,0},{80,16},{96,32},{112,48},{1... | collective-permute-start | bytes 1572872 | tf_op jit(solution)/shard_map/ppermute | solution.py:23
  7.9 24.6 %collective-permute-start.24 = (bf16[128,2048]{1,0:T(8,128)(2,1)}, bf16[128,2048]{1,0:T(8,128)(2,1)S(1)}, u32[]{:S(2)}, u32[]{:S(2)}) collective-permute-start(bf16[128,2048]{1,0:T(8,128)(2,1)} %bitcast.67), channel_id=1, source_target_pairs={{0,96},{16,112},{32,64},{48,80},{64,32},{80,48},{96,0},{112,16},{1... | collective-permute-start | bytes 1572872 | tf_op jit(solution)/shard_map/ppermute | solution.py:23
  38.1 22.2 %collective-permute-start.25 = (bf16[512,512]{1,0:T(8,128)(2,1)}, bf16[512,512]{1,0:T(8,128)(2,1)S(1)}, u32[]{:S(2)}, u32[]{:S(2)}) collective-permute-start(bf16[512,512]{1,0:T(8,128)(2,1)} %shard_map.125), channel_id=1, source_target_pairs={{0,128},{128,0},{1,129},{129,1},{2,130},{130,2},{3,131},{131,3},{4... | collective-permute-start | bytes 1572872 | tf_op jit(solution)/shard_map/ppermute | solution.py:27
  40.5 54.5 %collective-permute-start.14 = (bf16[256,2048]{1,0:T(8,128)(2,1)S(1)}, bf16[256,2048]{1,0:T(8,128)(2,1)S(1)}, u32[]{:S(2)}, u32[]{:S(2)}) collective-permute-start(bf16[256,2048]{1,0:T(8,128)(2,1)S(1)} %bitcast.32), channel_id=1, source_target_pairs={{0,17},{1,16},{2,19},{3,18},{4,21},{5,20},{6,23},{7,22},{8,25},{9,... | collective-permute-start | bytes 3145736 | tf_op jit(solution)/shard_map/ppermute | solution.py:37
  44.9 13.8 %collective-permute-start.6 = (bf16[2,128,512]{2,1,0:T(8,128)(2,1)}, bf16[2,128,512]{2,1,0:T(8,128)(2,1)S(1)}, u32[]{:S(2)}, u32[]{:S(2)}) collective-permute-start(bf16[2,128,512]{2,1,0:T(8,128)(2,1)} %get-tuple-element.55), channel_id=1, source_target_pairs={{0,32},{16,48},{32,0},{48,16},{64,96},{80,112},{96,64},{112,80},{1... | collective-permute-start | bytes 786440 | tf_op jit(solution)/shard_map/ppermute | solution.py:23
  47.4 10.6 %collective-permute-start.5 = (bf16[1,128,512]{2,1,0:T(8,128)(2,1)S(1)}, bf16[1,128,512]{2,1,0:T(8,128)(2,1)S(1)}, u32[]{:S(2)}, u32[]{:S(2)}) collective-permute-start(bf16[1,128,512]{2,1,0:T(8,128)(2,1)S(1)} %copy-done.40), channel_id=1, source_target_pairs={{0,96},{16,112},{32,64},{48,80},{64,32},{80,48},{96,0},{112,16},{1... | collective-permute-start | bytes 393224 | tf_op jit(solution)/shard_map/ppermute | solution.py:23
  58.0 13.6 %collective-permute-start.8 = (bf16[2,128,512]{2,1,0:T(8,128)(2,1)}, bf16[2,128,512]{2,1,0:T(8,128)(2,1)S(1)}, u32[]{:S(2)}, u32[]{:S(2)}) collective-permute-start(bf16[2,128,512]{2,1,0:T(8,128)(2,1)} %get-tuple-element.57), channel_id=1, source_target_pairs={{0,96},{16,112},{32,64},{48,80},{64,32},{80,48},{96,0},{112,16},{1... | collective-permute-start | bytes 786440 | tf_op jit(solution)/shard_map/ppermute | solution.py:23
  58.7 14.4 %collective-permute-start.9 = (bf16[2,128,512]{2,1,0:T(8,128)(2,1)}, bf16[2,128,512]{2,1,0:T(8,128)(2,1)S(1)}, u32[]{:S(2)}, u32[]{:S(2)}) collective-permute-start(bf16[2,128,512]{2,1,0:T(8,128)(2,1)} %get-tuple-element.54.refs_4_), channel_id=1, source_target_pairs={{0,16},{16,0},{32,48},{48,32},{64,80},{80,64},{96,112},{112,96},{1... | collective-permute-start | bytes 786440 | tf_op jit(solution)/shard_map/ppermute | solution.py:23
  60.3 14.3 %collective-permute-start.10 = (bf16[2,128,512]{2,1,0:T(8,128)(2,1)S(1)}, bf16[2,128,512]{2,1,0:T(8,128)(2,1)S(1)}, u32[]{:S(2)}, u32[]{:S(2)}) collective-permute-start(bf16[2,128,512]{2,1,0:T(8,128)(2,1)S(1)} %collective-permute-done.6.refs_5_), channel_id=1, source_target_pairs={{0,16},{16,0},{32,48},{48,32},{64,80},{80,64},{96,112},{112,96},{1... | collective-permute-start | bytes 786440 | tf_op jit(solution)/shard_map/ppermute | solution.py:23
  64.7 38.3 %collective-permute-start.26 = (bf16[512,512]{1,0:T(8,128)(2,1)}, bf16[512,512]{1,0:T(8,128)(2,1)S(1)}, u32[]{:S(2)}, u32[]{:S(2)}) collective-permute-start(bf16[512,512]{1,0:T(8,128)(2,1)} %shard_map.126.refs_0_.refs_1_.refs_12_), channel_id=1, source_target_pairs={{0,32},{16,48},{32,0},{48,16},{64,96},{80,112},{96,64},{112,80},{1... | collective-permute-start | bytes 1572872 | tf_op jit(solution)/shard_map/ppermute | solution.py:23
  73.1 13.0 %collective-permute-start.12 = (bf16[2,128,512]{2,1,0:T(8,128)(2,1)S(1)}, bf16[2,128,512]{2,1,0:T(8,128)(2,1)S(1)}, u32[]{:S(2)}, u32[]{:S(2)}) collective-permute-start(bf16[2,128,512]{2,1,0:T(8,128)(2,1)S(1)} %collective-permute-done.8.refs_7_), channel_id=1, source_target_pairs={{0,16},{16,0},{32,48},{48,32},{64,80},{80,64},{96,112},{112,96},{1... | collective-permute-start | bytes 786440 | tf_op jit(solution)/shard_map/ppermute | solution.py:23
  74.6 29.1 %collective-permute-start.27 = (bf16[512,512]{1,0:T(8,128)(2,1)}, bf16[512,512]{1,0:T(8,128)(2,1)S(1)}, u32[]{:S(2)}, u32[]{:S(2)}) collective-permute-start(bf16[512,512]{1,0:T(8,128)(2,1)} %shard_map.126.refs_0_.refs_1_.refs_12_), channel_id=1, source_target_pairs={{0,64},{16,80},{32,96},{48,112},{64,0},{80,16},{96,32},{112,48},{1... | collective-permute-start | bytes 1572872 | tf_op jit(solution)/shard_map/ppermute | solution.py:23
  80.5 24.6 %collective-permute-start.28 = (bf16[512,512]{1,0:T(8,128)(2,1)}, bf16[512,512]{1,0:T(8,128)(2,1)S(1)}, u32[]{:S(2)}, u32[]{:S(2)}) collective-permute-start(bf16[512,512]{1,0:T(8,128)(2,1)} %shard_map.126.refs_0_.refs_1_.refs_12_), channel_id=1, source_target_pairs={{0,96},{16,112},{32,64},{48,80},{64,32},{80,48},{96,0},{112,16},{1... | collective-permute-start | bytes 1572872 | tf_op jit(solution)/shard_map/ppermute | solution.py:23
  86.1 14.4 %collective-permute-start = (bf16[1,128,512]{2,1,0:T(8,128)(2,1)}, bf16[1,128,512]{2,1,0:T(8,128)(2,1)S(1)}, u32[]{:S(2)}, u32[]{:S(2)}) collective-permute-start(bf16[1,128,512]{2,1,0:T(8,128)(2,1)} %get-tuple-element.47), channel_id=1, source_target_pairs={{0,32},{16,48},{32,0},{48,16},{64,96},{80,112},{96,64},{112,80},{1... | collective-permute-start | bytes 393224 | tf_op jit(solution)/shard_map/ppermute | solution.py:23
  99.8 39.6 %collective-permute-start.15 = (bf16[512,512]{1,0:T(8,128)(2,1)}, bf16[512,512]{1,0:T(8,128)(2,1)S(1)}, u32[]{:S(2)}, u32[]{:S(2)}) collective-permute-start(bf16[512,512]{1,0:T(8,128)(2,1)} %get-tuple-element.60), channel_id=1, source_target_pairs={{0,32},{16,48},{32,0},{48,16},{64,96},{80,112},{96,64},{112,80},{1... | collective-permute-start | bytes 1572872 | tf_op jit(solution)/shard_map/ppermute | solution.py:23
  100.5 38.8 %collective-permute-start.16 = (bf16[512,512]{1,0:T(8,128)(2,1)}, bf16[512,512]{1,0:T(8,128)(2,1)S(1)}, u32[]{:S(2)}, u32[]{:S(2)}) collective-permute-start(bf16[512,512]{1,0:T(8,128)(2,1)} %get-tuple-element.61), channel_id=1, source_target_pairs={{0,64},{16,80},{32,96},{48,112},{64,0},{80,16},{96,32},{112,48},{1... | collective-permute-start | bytes 1572872 | tf_op jit(solution)/shard_map/ppermute | solution.py:23
  103.0 36.3 %collective-permute-start.17 = (bf16[512,512]{1,0:T(8,128)(2,1)}, bf16[512,512]{1,0:T(8,128)(2,1)S(1)}, u32[]{:S(2)}, u32[]{:S(2)}) collective-permute-start(bf16[512,512]{1,0:T(8,128)(2,1)} %get-tuple-element.62), channel_id=1, source_target_pairs={{0,96},{16,112},{32,64},{48,80},{64,32},{80,48},{96,0},{112,16},{1... | collective-permute-start | bytes 1572872 | tf_op jit(solution)/shard_map/ppermute | solution.py:23
  103.7 24.1 %collective-permute-start.1 = (bf16[1,128,512]{2,1,0:T(8,128)(2,1)S(1)}, bf16[1,128,512]{2,1,0:T(8,128)(2,1)S(1)}, u32[]{:S(2)}, u32[]{:S(2)}) collective-permute-start(bf16[1,128,512]{2,1,0:T(8,128)(2,1)S(1)} %copy-done.39), channel_id=1, source_target_pairs={{0,64},{16,80},{32,96},{48,112},{64,0},{80,16},{96,32},{112,48},{1... | collective-permute-start | bytes 393224 | tf_op jit(solution)/shard_map/ppermute | solution.py:23
  105.1 32.4 %collective-permute-start.2 = (bf16[1,128,512]{2,1,0:T(8,128)(2,1)S(1)}, bf16[1,128,512]{2,1,0:T(8,128)(2,1)S(1)}, u32[]{:S(2)}, u32[]{:S(2)}) collective-permute-start(bf16[1,128,512]{2,1,0:T(8,128)(2,1)S(1)} %copy-done.38), channel_id=1, source_target_pairs={{0,96},{16,112},{32,64},{48,80},{64,32},{80,48},{96,0},{112,16},{1... | collective-permute-start | bytes 393224 | tf_op jit(solution)/shard_map/ppermute | solution.py:23
  127.8 18.7 %collective-permute-start.29 = (bf16[2,512,256]{2,1,0:T(8,128)(2,1)}, bf16[2,512,256]{2,1,0:T(8,128)(2,1)S(1)}, u32[]{:S(2)}, u32[]{:S(2)}) collective-permute-start(bf16[2,512,256]{2,1,0:T(8,128)(2,1)} %get-tuple-element.68), channel_id=1, source_target_pairs={{0,16},{16,0},{32,48},{48,32},{64,80},{80,64},{96,112},{112,96},{1... | collective-permute-start | bytes 1572872 | tf_op jit(solution)/shard_map/ppermute | solution.py:23
  137.5 15.2 %collective-permute-start.30 = (bf16[2,512,256]{2,1,0:T(8,128)(2,1)}, bf16[2,512,256]{2,1,0:T(8,128)(2,1)S(1)}, u32[]{:S(2)}, u32[]{:S(2)}) collective-permute-start(bf16[2,512,256]{2,1,0:T(8,128)(2,1)} %get-tuple-element.73), channel_id=1, source_target_pairs={{0,16},{16,0},{32,48},{48,32},{64,80},{80,64},{96,112},{112,96},{1... | collective-permute-start | bytes 1572872 | tf_op jit(solution)/shard_map/ppermute | solution.py:23
  143.5 15.9 %collective-permute-start.18 = (bf16[512,512]{1,0:T(8,128)(2,1)}, bf16[512,512]{1,0:T(8,128)(2,1)S(1)}, u32[]{:S(2)}, u32[]{:S(2)}) collective-permute-start(bf16[512,512]{1,0:T(8,128)(2,1)} %shard_map.123.hid), channel_id=1, source_target_pairs={{0,128},{128,0},{1,129},{129,1},{2,130},{130,2},{3,131},{131,3},{4... | collective-permute-start | bytes 1572872 | tf_op jit(solution)/shard_map/ppermute | solution.py:27
  149.7 24.2 %collective-permute-start.31 = (bf16[4,128,256]{2,1,0:T(8,128)(2,1)}, bf16[4,128,256]{2,1,0:T(8,128)(2,1)S(1)}, u32[]{:S(2)}, u32[]{:S(2)}) collective-permute-start(bf16[4,128,256]{2,1,0:T(8,128)(2,1)} %get-tuple-element.75), channel_id=1, source_target_pairs={{0,32},{16,48},{32,0},{48,16},{64,96},{80,112},{96,64},{112,80},{1... | collective-permute-start | bytes 786440 | tf_op jit(solution)/shard_map/ppermute | solution.py:23
  155.5 10.8 %collective-permute-start.34 = (bf16[2,128,256]{2,1,0:T(8,128)(2,1)}, bf16[2,128,256]{2,1,0:T(8,128)(2,1)S(1)}, u32[]{:S(2)}, u32[]{:S(2)}) collective-permute-start(bf16[2,128,256]{2,1,0:T(8,128)(2,1)} %get-tuple-element.78), channel_id=1, source_target_pairs={{0,64},{16,80},{32,96},{48,112},{64,0},{80,16},{96,32},{112,48},{1... | collective-permute-start | bytes 393224 | tf_op jit(solution)/shard_map/ppermute | solution.py:23
  159.4 16.0 %collective-permute-start.33 = (bf16[4,128,256]{2,1,0:T(8,128)(2,1)}, bf16[4,128,256]{2,1,0:T(8,128)(2,1)S(1)}, u32[]{:S(2)}, u32[]{:S(2)}) collective-permute-start(bf16[4,128,256]{2,1,0:T(8,128)(2,1)} %get-tuple-element.77), channel_id=1, source_target_pairs={{0,64},{16,80},{32,96},{48,112},{64,0},{80,16},{96,32},{112,48},{1... | collective-permute-start | bytes 786440 | tf_op jit(solution)/shard_map/ppermute | solution.py:23
  165.4 37.0 %collective-permute-start.21 = (bf16[128,2048]{1,0:T(8,128)(2,1)}, bf16[128,2048]{1,0:T(8,128)(2,1)S(1)}, u32[]{:S(2)}, u32[]{:S(2)}) collective-permute-start(bf16[128,2048]{1,0:T(8,128)(2,1)} %get-tuple-element.66), channel_id=1, source_target_pairs={{0,96},{16,112},{32,64},{48,80},{64,32},{80,48},{96,0},{112,16},{1... | collective-permute-start | bytes 1572872 | tf_op jit(solution)/shard_map/ppermute | solution.py:23
  166.3 36.1 %collective-permute-start.20 = (bf16[128,2048]{1,0:T(8,128)(2,1)}, bf16[128,2048]{1,0:T(8,128)(2,1)S(1)}, u32[]{:S(2)}, u32[]{:S(2)}) collective-permute-start(bf16[128,2048]{1,0:T(8,128)(2,1)} %get-tuple-element.65), channel_id=1, source_target_pairs={{0,64},{16,80},{32,96},{48,112},{64,0},{80,16},{96,32},{112,48},{1... | collective-permute-start | bytes 1572872 | tf_op jit(solution)/shard_map/ppermute | solution.py:23
  167.9 34.4 %collective-permute-start.19 = (bf16[128,2048]{1,0:T(8,128)(2,1)}, bf16[128,2048]{1,0:T(8,128)(2,1)S(1)}, u32[]{:S(2)}, u32[]{:S(2)}) collective-permute-start(bf16[128,2048]{1,0:T(8,128)(2,1)} %get-tuple-element.64), channel_id=1, source_target_pairs={{0,32},{16,48},{32,0},{48,16},{64,96},{80,112},{96,64},{112,80},{1... | collective-permute-start | bytes 1572872 | tf_op jit(solution)/shard_map/ppermute | solution.py:23
  173.9 29.6 %collective-permute-start.37 = (bf16[256,2048]{1,0:T(8,128)(2,1)}, bf16[256,2048]{1,0:T(8,128)(2,1)S(1)}, u32[]{:S(2)}, u32[]{:S(2)}) collective-permute-start(bf16[256,2048]{1,0:T(8,128)(2,1)} %get-tuple-element.85), channel_id=1, source_target_pairs={{0,16},{16,0},{32,48},{48,32},{64,80},{80,64},{96,112},{112,96},{1... | collective-permute-start | bytes 3145736 | tf_op jit(solution)/shard_map/ppermute | solution.py:23
  175.3 23.1 %collective-permute-start.35 = (bf16[4,128,256]{2,1,0:T(8,128)(2,1)S(1)}, bf16[4,128,256]{2,1,0:T(8,128)(2,1)S(1)}, u32[]{:S(2)}, u32[]{:S(2)}) collective-permute-start(bf16[4,128,256]{2,1,0:T(8,128)(2,1)S(1)} %copy-done.37), channel_id=1, source_target_pairs={{0,96},{16,112},{32,64},{48,80},{64,32},{80,48},{96,0},{112,16},{1... | collective-permute-start | bytes 786440 | tf_op jit(solution)/shard_map/ppermute | solution.py:23
  (48 other events, 301.8 us)
where the time goes:
time: 207 us; the launch traced here: 206 us
  waiting for transfers between devices  81.8 us (40%)
  Pallas kernels  64.6 us (31%)
  starting transfers between devices  48.1 us (23%)
  local copies, waits for them, and re-layouts  7.61 us (4%)
  other arithmetic  2.69 us (1%)
    ppermute x34, waiting for transfers between devices, seq_shift(): return lax.ppermute(value, 'seq', [(i, i ^ mask) for i in range(size)])  81.8 us
    pallas_call x16, Pallas kernels, call(): pl.pallas_call(body, out_shape=out_shapes, grid_spec=pltpu.PrefetchScalar...  64.6 us
    ppermute x34, starting transfers between devices, seq_shift(): return lax.ppermute(value, 'seq', [(i, i ^ mask) for i in range(size)])  39.2 us
    unnamed x84, local copies, waits for them, and re-layouts  7.61 us
    ppermute x2, starting transfers between devices, branch_swap(): return lax.ppermute(value, 'branch', [(0, 1), (1, 0)])  5.4 us
  transfers between devices with their start and end apart: 38, of which 12 were waited for; matrix products, arithmetic and copies ran while one was open for 1% of the time, Pallas kernels for 29%

commit v1 on v0

--- a/solution.py
+++ b/solution.py
@@ -27,14 +27,16 @@
     return lax.ppermute(value, "branch", [(0, 1), (1, 0)])
 
 
-def partner_rows(weight):
+def rep_shift(value, mask):
     seqs, reps = lax.axis_size("seq"), lax.axis_size("rep")
     pairs = [
-        (s * reps + r, (s ^ 1) * reps + (r ^ 1 if reps > 1 else r))
-        for s in range(seqs)
-        for r in range(reps)
+        (s * reps + r, (s ^ mask) * reps + (r ^ 1)) for s in range(seqs) for r in range(reps)
     ]
-    return lax.ppermute(weight, ("seq", "rep"), pairs)
+    return lax.ppermute(value, ("seq", "rep"), pairs)
+
+
+def half_rows(weight, odd_rep):
+    return lax.dynamic_slice(weight, (HEAD * (1 - odd_rep), 0), (HEAD, weight.shape[1]))
 
 
 def dot(left, right, left_dim, right_dim):
@@ -125,55 +127,62 @@
     )
 
 
+def split_specs():
+    return [
+        pl.BlockSpec((4 * TOK, CHUNK), lambda i, seq: (0, 0)),
+        pl.BlockSpec((4 * TOK, HEAD), lambda i, seq: (0, 2 + seq[1])),
+        pl.BlockSpec((4 * TOK, HEAD), lambda i, seq: (0, 3 - seq[1])),
+    ]
+
+
 def back_couple_product(seq, grads, couple):
-    def body(seq_ref, g0, g1, g2, g3, w0, w1, out):
+    def body(seq_ref, g0, g1, g2, g3, w0, w1, w2, out):
         rows = jnp.concatenate([g0[...], g1[...], g2[...], g3[...]], axis=0)
         out[:, :CHUNK] = dot(rows, w0[...], 1, 1).astype(BF16)
-        out[:, CHUNK:] = dot(rows, w1[...], 1, 1).astype(BF16)
-
-    specs = [full((TOK, 8 * CHUNK))] * 4 + [full((CHUNK, 8 * CHUNK))] * 2
+        out[:, CHUNK:] = dot(rows, jnp.concatenate([w1[...], w2[...]], axis=0), 1, 1).astype(BF16)
+
+    specs = [full((TOK, 8 * CHUNK))] * 4 + [full((CHUNK, 8 * CHUNK))]
+    specs = specs + [full((HEAD, 8 * CHUNK))] * 2
+    return call(
+        body, (1,), specs, full((4 * TOK, WIDE)), sds((4 * TOK, WIDE)), seq, (*grads, *couple)
+    )
+
+
+def grad_hidden_chunk(seq, grads, partner_back):
+    def body(seq_ref, *refs):
+        ins, backs, out = refs[:8], refs[8:11], refs[11]
+        for r in range(4):
+            rows = slice(r * TOK, (r + 1) * TOK)
+            low = ins[2 * r][...].astype(F32) + backs[0][rows].astype(F32)
+            out[rows, :CHUNK] = low.astype(BF16)
+            for p in range(2):
+                cols = slice(p * HEAD, (p + 1) * HEAD)
+                high = ins[2 * r + 1][:, cols].astype(F32) + backs[1 + p][rows].astype(F32)
+                out[rows, CHUNK + p * HEAD : CHUNK + (p + 1) * HEAD] = high.astype(BF16)
+
+    specs = [chunk_spec(TOK, h) for _ in range(4) for h in range(2)]
+    args = [grad for grad in grads for _ in range(2)]
     return call(
         body,
         (1,),
-        specs,
+        specs + split_specs(),
         full((4 * TOK, WIDE)),
         sds((4 * TOK, WIDE)),
         seq,
-        (*grads, *couple),
-    )
-
-
-def grad_hidden_chunk(seq, grads, partner_back):
-    def body(seq_ref, *refs):
-        ins, back, out = refs[:8], refs[8], refs[9]
-        for r in range(4):
-            for h in range(2):
-                rows = slice(r * TOK, (r + 1) * TOK)
-                cols = slice(h * CHUNK, (h + 1) * CHUNK)
-                total = ins[2 * r + h][...].astype(F32) + back[rows, cols].astype(F32)
-                out[rows, cols] = total.astype(BF16)
-
-    specs = [chunk_spec(TOK, h) for _ in range(4) for h in range(2)]
-    args = [grad for grad in grads for _ in range(2)]
-    return call(
-        body,
-        (1,),
-        specs + [full((4 * TOK, WIDE))],
-        full((4 * TOK, WIDE)),
-        sds((4 * TOK, WIDE)),
-        seq,
-        (*args, partner_back),
-    )
-
-
-def proj_specs():
-    return [chunk_spec(CHUNK, rel) for _ in range(2) for rel in range(8)]
+        (*args, *([partner_back] * 3)),
+    )
+
+
+def head_at(j, seq):
+    return j ^ (seq[1] & (j >> 1))
 
 
 def head_specs(first):
-    query = pl.BlockSpec((None, TOK, HEAD), lambda j, seq: (0, 0, j + first))
-    pair = pl.BlockSpec((2, TOK, HEAD), lambda j, seq: (0, 0, j + first))
-    other = pl.BlockSpec((2, TOK, HEAD), lambda j, seq: (0, 0, (j + first + 2) % 4))
+    at = lambda j, seq: (0, 0, head_at(j + first, seq))
+    swapped = lambda j, seq: (0, 0, head_at(j + first, seq) ^ 2)
+    query = pl.BlockSpec((None, TOK, HEAD), at)
+    pair = pl.BlockSpec((2, TOK, HEAD), at)
+    other = pl.BlockSpec((2, TOK, HEAD), swapped)
     return [query] * 4 + [pair] * 4 + [other] * 4
 
 
@@ -210,11 +219,12 @@
 
 def output_partial(seq, attended, proj):
     def body(seq_ref, att, *refs):
-        weights, outs = refs[:16], refs[16:]
+        weights, outs = refs[:24], refs[24:]
         first, second = att[:, :CHUNK], att[:, CHUNK:]
         for rel in range(8):
             dest, half = rel >> 1, rel & 1
-            part = dot(first, weights[rel][...], 1, 0) + dot(second, weights[8 + rel][...], 1, 0)
+            held = jnp.concatenate([weights[8 + rel][...], weights[16 + rel][...]], axis=0)
+            part = dot(first, weights[rel][...], 1, 0) + dot(second, held, 1, 0)
             for r in range(4):
                 rows = (r ^ dest) * TOK
                 outs[dest][rows : rows + TOK, half * CHUNK : (half + 1) * CHUNK] = part[
@@ -224,11 +234,12 @@
     return call(
         body,
         (1,),
-        [full((4 * TOK, WIDE))] + proj_specs(),
+        [full((4 * TOK, WIDE))]
+        + [chunk_spec(rows, rel) for rows in (CHUNK, HEAD, HEAD) for rel in range(8)],
         [full((4 * TOK, WIDE))] * 4,
         [sds((4 * TOK, WIDE), F32)] + [sds((4 * TOK, WIDE))] * 3,
         seq,
-        (attended, *([proj[0]] * 8), *([proj[1]] * 8)),
+        (attended, *[weight for weight in proj for _ in range(8)]),
     )
 
 
@@ -253,8 +264,10 @@
 
 
 def mixed_partial(seq, partner_hidden, hidden, couple):
-    def body(seq_ref, ph, hid, w0, w1, o0, o1, o2, o3):
-        part = dot(ph[:, :CHUNK], w0[...], 1, 0) + dot(ph[:, CHUNK:], w1[...], 1, 0)
+    def body(seq_ref, p0, p1, p2, hid, w0, w1, w2, o0, o1, o2, o3):
+        held = jnp.concatenate([w1[...], w2[...]], axis=0)
+        part = dot(p0[...], w0[...], 1, 0)
+        part = part + dot(jnp.concatenate([p1[...], p2[...]], axis=1), held, 1, 0)
         first = pl.program_id(0) == 0
         odd = (seq_ref[0] & 1) == 1
         outs = (o0, o1, o2, o3)
@@ -278,11 +291,13 @@
     return call(
         body,
         (4,),
-        [full((4 * TOK, WIDE))] * 2 + [wide_cols(CHUNK)] * 2,
+        split_specs()
+        + [full((4 * TOK, WIDE))]
+        + [wide_cols(rows) for rows in (CHUNK, HEAD, HEAD)],
         [wide_cols(TOK)] * 4,
         [sds((TOK, 8 * CHUNK), F32)] + [sds((TOK, 8 * CHUNK))] * 3,
         seq,
-        (partner_hidden, hidden, *couple),
+        (*([partner_hidden] * 3), hidden, *couple),
     )
 
 
@@ -305,9 +320,12 @@
 
 
 def backward_half(seq, heads, grad_chunks, proj_rows, half):
+    count = len(proj_rows)
+    at = lambda j, seq: head_at(j + 2 * half, seq) & 1
+
     def body(seq_ref, *refs):
-        chunks, weights = refs[12:16], refs[16:24]
-        dq_out, kv_own, kv_other, grad_att = refs[24:28]
+        chunks, weights = refs[12:16], refs[16 : 16 + 8 * count]
+        dq_out, kv_own, kv_other, grad_att = refs[16 + 8 * count :]
         step = pl.program_id(0)
 
         @pl.when(step == 0)
@@ -319,7 +337,8 @@
                 )
                 for h in range(2):
                     piece = rows[:, h * CHUNK : (h + 1) * CHUNK]
-                    term = dot(piece, weights[2 * d + h][...], 1, 1)
+                    blocks = [weights[8 * w + 2 * d + h][...] for w in range(count)]
+                    term = dot(piece, jnp.concatenate(blocks, axis=0), 1, 1)
                     total = term if total is None else total + term
             grad_att[0] = total[:, :HEAD].astype(BF16)
             grad_att[1] = total[:, HEAD:].astype(BF16)
@@ -340,17 +359,17 @@
         kv_other[0] = d_key[rows:]
         kv_other[1] = d_value[rows:]
 
-    pair = pl.BlockSpec((2, 4 * TOK, HEAD), lambda j, seq: (0, 0, j))
+    pair = pl.BlockSpec((2, 4 * TOK, HEAD), lambda j, seq: (0, 0, at(j, seq)))
     return call(
         body,
         (2,),
         head_specs(2 * half)
         + [full((4 * TOK, WIDE))] * 4
-        + [chunk_spec(CHUNK, rel) for rel in range(8)],
-        [pl.BlockSpec((4 * TOK, HEAD), lambda j, seq: (0, j)), pair, pair],
+        + [chunk_spec(weight.shape[0], rel) for weight in proj_rows for rel in range(8)],
+        [pl.BlockSpec((4 * TOK, HEAD), lambda j, seq: (0, at(j, seq))), pair, pair],
         [sds((4 * TOK, CHUNK))] + [sds((2, 4 * TOK, CHUNK))] * 2,
         seq,
-        (*heads, *grad_chunks, *([proj_rows] * 8)),
+        (*heads, *grad_chunks, *[weight for weight in proj_rows for _ in range(8)]),
         scratch=[pltpu.VMEM((2, 4 * TOK, HEAD), BF16)],
     )
 
@@ -390,16 +409,18 @@
 
 
 def steps(queries, key_vecs, value_vecs, hidden_in, out_proj, couple_proj, grad_mixed):
-    seq = lax.axis_index("seq").astype(jnp.int32).reshape(1)
+    odd_rep = lax.axis_index("rep").astype(jnp.int32) & 1
+    seq = jnp.stack([lax.axis_index("seq").astype(jnp.int32), odd_rep])
+    proj_half = rep_shift(half_rows(out_proj[0], odd_rep), 1)
+    couple_half = rep_shift(half_rows(couple_proj[0], odd_rep), 1)
     pairs = relative_columns(seq, (key_vecs[0], value_vecs[0]))
     pairs = exchange(pairs)
     others = [seq_shift(pairs[r], 1) for r in range(4)]
     items = exchange(relative_columns(seq, (queries[0],)))
     grads = exchange([grad_mixed[0]] * 4)
-    couple = (couple_proj[0], partner_rows(couple_proj[0]))
     inputs = exchange(relative_columns(seq, (hidden_in[0],)))
-    late_proj, _ = lax.optimization_barrier((out_proj[0], couple[1]))
-    proj = (out_proj[0], partner_rows(late_proj))
+    proj = (out_proj[0], proj_half, rep_shift(proj_half, 0))
+    couple = (couple_proj[0], couple_half, rep_shift(couple_half, 0))
     heads = (*items, *pairs, *others)
 
     back = back_couple_product(seq, grads, couple)
@@ -409,9 +430,9 @@
 
     sums = exchange(output_partial(seq, attend(seq, heads), proj))
 
-    first = backward_half(seq, heads, chunks, proj[0], 0)
+    first = backward_half(seq, heads, chunks, proj[:1], 0)
     got_high = seq_shift(first[2], 1)
-    second = backward_half(seq, heads, chunks, proj[1], 1)
+    second = backward_half(seq, heads, chunks, proj[1:], 1)
     got_low = seq_shift(second[2], 1)
 
     hidden = hidden_sum(seq, inputs, sums[0], sums[1:])
@@ -427,9 +448,7 @@
     def chunk_half(r, h):
         return (chunks[r], pl.BlockSpec((TOK, CHUNK), lambda i, seq: (r, h)))
 
-    (grad_hid,) = absolute_columns(
-        seq, [[(chunk_half(r, 0), chunk_half(r, 1))] for r in range(4)]
-    )
+    (grad_hid,) = absolute_columns(seq, [[(chunk_half(r, 0), chunk_half(r, 1))] for r in range(4)])
     mixed = mixed_parts[0]
     for part in mixed_parts[1:]:
         mixed = mixed + part.astype(F32)

time: 207 us -> 231 us (1.12)
  the two profiles are of different devices: /device:TPU:1 before, /device:TPU:160 now
where the time goes in v1:
time: 231 us; the launch traced here: 230 us
  waiting for transfers between devices  92.1 us (40%)
  Pallas kernels  76.6 us (33%)
  starting transfers between devices  52.2 us (23%)
  local copies, waits for them, and re-layouts  5.14 us (2%)
  other arithmetic  3.42 us (1%)
    ppermute x34, waiting for transfers between devices, seq_shift(): return lax.ppermute(value, 'seq', [(i, i ^ mask) for i in range(size)])  92.1 us
    pallas_call x16, Pallas kernels, call(): pl.pallas_call(body, out_shape=out_shapes, grid_spec=pltpu.PrefetchScalar...  76.6 us
    ppermute x34, starting transfers between devices, seq_shift(): return lax.ppermute(value, 'seq', [(i, i ^ mask) for i in range(size)])  46.7 us
    ppermute x4, starting transfers between devices, rep_shift(): return lax.ppermute(value, ('seq', 'rep'), pairs)  5.44 us
    unnamed x92, local copies, waits for them, and re-layouts  5.07 us
  transfers between devices with their start and end apart: 40, of which 20 were waited for; matrix products, arithmetic and copies ran while one was open for 1% of the time, Pallas kernels for 32%

profile of v1, /device:TPU:160, one launch (start us, length us, event | category | flops | bytes accessed | tf_op | source)
XLA Modules:
  0.0 230.3 jit_solution(15660221835442175276)
XLA Ops:
  5.5 2.9 %collective-permute-start.4 = (bf16[1,128,512]{2,1,0:T(8,128)(2,1)}, bf16[1,128,512]{2,1,0:T(8,128)(2,1)S(1)}, u32[]{:S(2)}, u32[]{:S(2)}) collective-permute-start(bf16[1,128,512]{2,1,0:T(8,128)(2,1)} %get-tuple-element.51), channel_id=1, source_target_pairs={{0,64},{16,80},{32,96},{48,112},{64,0},{80,16},{96,32},{112,48},{1... | collective-permute-start | bytes 393224 | tf_op jit(solution)/shard_map/ppermute | solution.py:23
  8.5 2.8 %collective-permute-start.19 = (bf16[128,2048]{1,0:T(8,128)(2,1)S(1)}, bf16[128,2048]{1,0:T(8,128)(2,1)S(1)}, u32[]{:S(2)}, u32[]{:S(2)}) collective-permute-start(bf16[128,2048]{1,0:T(8,128)(2,1)S(1)} %dynamic-slice_bitcast_fusion), channel_id=1, source_target_pairs={{0,17},{1,16},{2,19},{3,18},{4,21},{5,20},{6,23},{7,22},{8,25},{9,... | collective-permute-start | bytes 1572872 | tf_op jit(solution)/shard_map/ppermute | solution.py:35
  11.6 3.0 %shard_map.120 = (bf16[2,128,512]{2,1,0:T(8,128)(2,1)}, bf16[2,128,512]{2,1,0:T(8,128)(2,1)}, bf16[2,128,512]{2,1,0:T(8,128)(2,1)}, bf16[2,128,512]{2,1,0:T(8,128)(2,1)}) custom-call(s32[2]{0:T(128)} %pad_add_fusion.seq_ref, bf16[128,2048]{1,0:T(8,128)(2,1)} %bitcast.45, bf16[128,2048]{1,0:T(8,128)(2,1)} %bitcast.46, bf16[128,2048]{1,0:T(8,128)(2,1)} %bitcast.47, ...), custom_call_target="tpu_custom_call" | custom-call | tf_op jit(solution)/shard_map/pallas_call | solution.py:53
  15.0 4.1 %collective-permute-start.7 = (bf16[2,128,512]{2,1,0:T(8,128)(2,1)}, bf16[2,128,512]{2,1,0:T(8,128)(2,1)S(1)}, u32[]{:S(2)}, u32[]{:S(2)}) collective-permute-start(bf16[2,128,512]{2,1,0:T(8,128)(2,1)} %get-tuple-element.55), channel_id=1, source_target_pairs={{0,64},{16,80},{32,96},{48,112},{64,0},{80,16},{96,32},{112,48},{1... | collective-permute-start | bytes 786440 | tf_op jit(solution)/shard_map/ppermute | solution.py:23
  19.9 4.0 %collective-permute-done.6.refs_5_ = bf16[2,128,512]{2,1,0:T(8,128)(2,1)S(1)} collective-permute-done((bf16[2,128,512]{2,1,0:T(8,128)(2,1)}, bf16[2,128,512]{2,1,0:T(8,128)(2,1)S(1)}, u32[]{:S(2)}, u32[]{:S(2)}) %collective-permute-start.6) | collective-permute-done | bytes 262176 | tf_op jit(solution)/shard_map/ppermute | solution.py:23
  24.0 8.1 %collective-permute-done.7.refs_6_ = bf16[2,128,512]{2,1,0:T(8,128)(2,1)S(1)} collective-permute-done((bf16[2,128,512]{2,1,0:T(8,128)(2,1)}, bf16[2,128,512]{2,1,0:T(8,128)(2,1)S(1)}, u32[]{:S(2)}, u32[]{:S(2)}) %collective-permute-start.7) | collective-permute-done | bytes 262176 | tf_op jit(solution)/shard_map/ppermute | solution.py:23
  36.2 4.7 %collective-permute-done.24.g1.refs_2_.refs_3_ = bf16[128,2048]{1,0:T(8,128)(2,1)S(1)} collective-permute-done((bf16[128,2048]{1,0:T(8,128)(2,1)S(1)}, bf16[128,2048]{1,0:T(8,128)(2,1)S(1)}, u32[]{:S(2)}, u32[]{:S(2)}) %collective-permute-start.24) | collective-permute-done | bytes 524320 | tf_op jit(solution)/shard_map/ppermute | solution.py:23
  41.7 10.7 %collective-permute-done.25.g2.refs_4_.refs_5_ = bf16[128,2048]{1,0:T(8,128)(2,1)S(1)} collective-permute-done((bf16[128,2048]{1,0:T(8,128)(2,1)S(1)}, bf16[128,2048]{1,0:T(8,128)(2,1)S(1)}, u32[]{:S(2)}, u32[]{:S(2)}) %collective-permute-start.25) | collective-permute-done | bytes 524320 | tf_op jit(solution)/shard_map/ppermute | solution.py:23
  59.3 4.9 %shard_map.125 = bf16[512,512]{1,0:T(8,128)(2,1)} custom-call(s32[2]{0:T(128)} %pad_add_fusion.seq_ref, bf16[128,2048]{1,0:T(8,128)(2,1)} %bitcast.69, bf16[128,2048]{1,0:T(8,128)(2,1)} %copy-done.7, bf16[128,2048]{1,0:T(8,128)(2,1)} %copy-done.8, bf16[128,2048]{1,0:T(8,128)(2,1)} %copy-done.9, bf16[256,2048]{1,0:T(8,128)(2,1)} %bitcast.76, ...), custom_call_target="tpu_custom_call" | custom-call | tf_op jit(solution)/shard_map/pallas_call | solution.py:53
  65.7 5.6 %collective-permute-done.10.refs_9_ = bf16[2,128,512]{2,1,0:T(8,128)(2,1)S(1)} collective-permute-done((bf16[2,128,512]{2,1,0:T(8,128)(2,1)S(1)}, bf16[2,128,512]{2,1,0:T(8,128)(2,1)S(1)}, u32[]{:S(2)}, u32[]{:S(2)}) %collective-permute-start.10) | collective-permute-done | bytes 262176 | tf_op jit(solution)/shard_map/ppermute | solution.py:23
  71.4 3.1 %collective-permute-done.11.refs_10_ = bf16[2,128,512]{2,1,0:T(8,128)(2,1)S(1)} collective-permute-done((bf16[2,128,512]{2,1,0:T(8,128)(2,1)S(1)}, bf16[2,128,512]{2,1,0:T(8,128)(2,1)S(1)}, u32[]{:S(2)}, u32[]{:S(2)}) %collective-permute-start.11) | collective-permute-done | bytes 262176 | tf_op jit(solution)/shard_map/ppermute | solution.py:23
  74.4 2.8 %collective-permute-done.12.refs_11_ = bf16[2,128,512]{2,1,0:T(8,128)(2,1)S(1)} collective-permute-done((bf16[2,128,512]{2,1,0:T(8,128)(2,1)S(1)}, bf16[2,128,512]{2,1,0:T(8,128)(2,1)S(1)}, u32[]{:S(2)}, u32[]{:S(2)}) %collective-permute-start.12) | collective-permute-done | bytes 262176 | tf_op jit(solution)/shard_map/ppermute | solution.py:23
  78.0 9.2 %shard_map.121.att = bf16[512,512]{1,0:T(8,128)(2,1)} custom-call(s32[2]{0:T(128)} %pad_add_fusion.seq_ref, bf16[1,128,512]{2,1,0:T(8,128)(2,1)} %get-tuple-element.49.refs_0_, bf16[1,128,512]{2,1,0:T(8,128)(2,1)} %copy-done.26, bf16[1,128,512]{2,1,0:T(8,128)(2,1)} %copy-done.27, bf16[1,128,512]{2,1,0:T(8,128)(2,1)} %copy-done.28, ...), custom_call_target="tpu_custom_call" | custom-call | tf_op jit(solution)/shard_map/pallas_call | solution.py:53
  88.0 4.5 %shard_map.122 = (f32[512,512]{1,0:T(8,128)}, bf16[512,512]{1,0:T(8,128)(2,1)}, bf16[512,512]{1,0:T(8,128)(2,1)}, bf16[512,512]{1,0:T(8,128)(2,1)}) custom-call(s32[2]{0:T(128)} %pad_add_fusion.seq_ref, bf16[512,512]{1,0:T(8,128)(2,1)} %shard_map.121.att, bf16[256,2048]{1,0:T(8,128)(2,1)} %bitcast.21, bf16[256,2048]{1,0:T(8,128)(2,1)} %bitcast.22, ...), custom_call_target="tpu_custom_call" | custom-call | tf_op jit(solution)/shard_map/pallas_call | solution.py:53
  100.8 9.6 %collective-permute-done.i1 = bf16[1,128,512]{2,1,0:T(8,128)(2,1)S(1)} collective-permute-done((bf16[1,128,512]{2,1,0:T(8,128)(2,1)}, bf16[1,128,512]{2,1,0:T(8,128)(2,1)S(1)}, u32[]{:S(2)}, u32[]{:S(2)}) %collective-permute-start) | collective-permute-done | bytes 131104 | tf_op jit(solution)/shard_map/ppermute | solution.py:23
  113.9 2.9 %shard_map.126.refs_0_.refs_1_.refs_12_ = bf16[512,512]{1,0:T(8,128)(2,1)} custom-call(s32[2]{0:T(128)} %pad_add_fusion.seq_ref, bf16[128,2048]{1,0:T(8,128)(2,1)} %bitcast.70, bf16[128,2048]{1,0:T(8,128)(2,1)} %bitcast.71, bf16[128,2048]{1,0:T(8,128)(2,1)} %copy-done.7, bf16[128,2048]{1,0:T(8,128)(2,1)} %copy-done.7, bf16[128,2048]{1,0:T(8,128)(2,1)} %copy-done.8, ...), custom_call_target="tpu_custom_call" | custom-call | tf_op jit(solution)/shard_map/pallas_call | solution.py:53
  116.8 8.6 %collective-permute-done.1.i2 = bf16[1,128,512]{2,1,0:T(8,128)(2,1)S(1)} collective-permute-done((bf16[1,128,512]{2,1,0:T(8,128)(2,1)}, bf16[1,128,512]{2,1,0:T(8,128)(2,1)S(1)}, u32[]{:S(2)}, u32[]{:S(2)}) %collective-permute-start.1) | collective-permute-done | bytes 131104 | tf_op jit(solution)/shard_map/ppermute | solution.py:23
  126.8 3.4 %collective-permute-start.30 = (bf16[512,512]{1,0:T(8,128)(2,1)}, bf16[512,512]{1,0:T(8,128)(2,1)S(1)}, u32[]{:S(2)}, u32[]{:S(2)}) collective-permute-start(bf16[512,512]{1,0:T(8,128)(2,1)} %shard_map.126.refs_0_.refs_1_.refs_12_), channel_id=1, source_target_pairs={{0,96},{16,112},{32,64},{48,80},{64,32},{80,48},{96,0},{112,16},{1... | collective-permute-start | bytes 1572872 | tf_op jit(solution)/shard_map/ppermute | solution.py:23
  131.1 3.6 %shard_map.123.hid = bf16[512,512]{1,0:T(8,128)(2,1)} custom-call(s32[2]{0:T(128)} %pad_add_fusion.seq_ref, bf16[1,128,512]{2,1,0:T(8,128)(2,1)} %get-tuple-element.45.i0, bf16[1,128,512]{2,1,0:T(8,128)(2,1)} %copy-done.38, bf16[1,128,512]{2,1,0:T(8,128)(2,1)} %copy-done.39, bf16[1,128,512]{2,1,0:T(8,128)(2,1)} %copy-done.40, ...), custom_call_target="tpu_custom_call" | custom-call | tf_op jit(solution)/shard_map/pallas_call | solution.py:53
  136.3 7.7 %collective-permute-done.29.refs_4_.refs_5_.refs_14_ = bf16[512,512]{1,0:T(8,128)(2,1)S(1)} collective-permute-done((bf16[512,512]{1,0:T(8,128)(2,1)}, bf16[512,512]{1,0:T(8,128)(2,1)S(1)}, u32[]{:S(2)}, u32[]{:S(2)}) %collective-permute-start.29) | collective-permute-done | bytes 524320 | tf_op jit(solution)/shard_map/ppermute | solution.py:23
  144.1 5.9 %collective-permute-done.30.refs_6_.refs_7_.refs_15_ = bf16[512,512]{1,0:T(8,128)(2,1)S(1)} collective-permute-done((bf16[512,512]{1,0:T(8,128)(2,1)}, bf16[512,512]{1,0:T(8,128)(2,1)S(1)}, u32[]{:S(2)}, u32[]{:S(2)}) %collective-permute-start.30) | collective-permute-done | bytes 524320 | tf_op jit(solution)/shard_map/ppermute | solution.py:23
  150.8 9.1 %shard_map.128 = (bf16[512,256]{1,0:T(8,128)(2,1)}, bf16[2,512,256]{2,1,0:T(8,128)(2,1)}, bf16[2,512,256]{2,1,0:T(8,128)(2,1)}) custom-call(s32[2]{0:T(128)} %pad_add_fusion.seq_ref, bf16[1,128,512]{2,1,0:T(8,128)(2,1)} %get-tuple-element.49.refs_0_, bf16[1,128,512]{2,1,0:T(8,128)(2,1)} %copy-done.26, bf16[1,128,512]{2,1,0:T(8,128)(2,1)} %copy-done.27, ...), custom_call_target="tpu_custom_call" | custom-call | tf_op jit(solution)/shard_map/pallas_call | solution.py:53
  163.0 6.0 %shard_map.124 = (f32[128,2048]{1,0:T(8,128)}, bf16[128,2048]{1,0:T(8,128)(2,1)}, bf16[128,2048]{1,0:T(8,128)(2,1)}, bf16[128,2048]{1,0:T(8,128)(2,1)}) custom-call(s32[2]{0:T(128)} %pad_add_fusion.seq_ref, bf16[512,512]{1,0:T(8,128)(2,1)} %copy-done.10, bf16[512,512]{1,0:T(8,128)(2,1)} %copy-done.10, bf16[512,512]{1,0:T(8,128)(2,1)} %copy-done.10, ...), custom_call_target="tpu_custom_call" | custom-call | tf_op jit(solution)/shard_map/pallas_call | solution.py:53
  169.3 9.2 %shard_map.129 = (bf16[512,256]{1,0:T(8,128)(2,1)}, bf16[2,512,256]{2,1,0:T(8,128)(2,1)}, bf16[2,512,256]{2,1,0:T(8,128)(2,1)}) custom-call(s32[2]{0:T(128)} %pad_add_fusion.seq_ref, bf16[1,128,512]{2,1,0:T(8,128)(2,1)} %get-tuple-element.49.refs_0_, bf16[1,128,512]{2,1,0:T(8,128)(2,1)} %copy-done.26, bf16[1,128,512]{2,1,0:T(8,128)(2,1)} %copy-done.27, ...), custom_call_target="tpu_custom_call" | custom-call | tf_op jit(solution)/shard_map/pallas_call | solution.py:53
  183.9 5.8 %shard_map.133 = (f32[256,2048]{1,0:T(8,128)}, bf16[256,2048]{1,0:T(8,128)(2,1)}) custom-call(s32[2]{0:T(128)} %pad_add_fusion.seq_ref, bf16[512,512]{1,0:T(8,128)(2,1)} %copy-done.10, bf16[128,2048]{1,0:T(8,128)(2,1)} %bitcast.72, bf16[128,2048]{1,0:T(8,128)(2,1)} %copy-done.7, bf16[128,2048]{1,0:T(8,128)(2,1)} %copy-done.8, bf16[128,2048]{1,0:T(8,128)(2,1)} %copy-done.9), custom_call_target="tpu_custom_call" | custom-call | tf_op jit(solution)/shard_map/pallas_call | solution.py:53
  191.8 2.7 %shard_map.131 = (bf16[2,128,256]{2,1,0:T(8,128)(2,1)}, bf16[2,128,256]{2,1,0:T(8,128)(2,1)}, bf16[2,128,256]{2,1,0:T(8,128)(2,1)}, bf16[2,128,256]{2,1,0:T(8,128)(2,1)}) custom-call(s32[2]{0:T(128)} %pad_add_fusion.seq_ref, bf16[2,512,256]{2,1,0:T(8,128)(2,1)} %get-tuple-element.70.a, bf16[2,512,256]{2,1,0:T(8,128)(2,1)} %copy-done.34), custom_call_target="tpu_custom_call" | custom-call | tf_op jit(solution)/shard_map/pallas_call | solution.py:53
  196.4 3.2 %shard_map.127 = bf16[128,2048]{1,0:T(8,128)(2,1)} custom-call(s32[2]{0:T(128)} %pad_add_fusion.seq_ref, bf16[512,512]{1,0:T(8,128)(2,1)} %shard_map.126.refs_0_.refs_1_.refs_12_, bf16[512,512]{1,0:T(8,128)(2,1)} %shard_map.126.refs_0_.refs_1_.refs_12_, bf16[512,512]{1,0:T(8,128)(2,1)} %copy-done.3, bf16[512,512]{1,0:T(8,128)(2,1)} %copy-done.3, ...), custom_call_target="tpu_custom_call" | custom-call | tf_op jit(solution)/shard_map/pallas_call | solution.py:53
  199.6 3.0 %shard_map.130 = (bf16[4,128,256]{2,1,0:T(8,128)(2,1)}, bf16[4,128,256]{2,1,0:T(8,128)(2,1)}, bf16[4,128,256]{2,1,0:T(8,128)(2,1)}, bf16[4,128,256]{2,1,0:T(8,128)(2,1)}) custom-call(s32[2]{0:T(128)} %pad_add_fusion.seq_ref, bf16[2,512,256]{2,1,0:T(8,128)(2,1)} %get-tuple-element.65.a, bf16[2,512,256]{2,1,0:T(8,128)(2,1)} %copy-done.33, ...), custom_call_target="tpu_custom_call" | custom-call | tf_op jit(solution)/shard_map/pallas_call | solution.py:53
  204.7 3.2 %collective-permute-done.21 = bf16[128,2048]{1,0:T(8,128)(2,1)S(1)} collective-permute-done((bf16[128,2048]{1,0:T(8,128)(2,1)S(1)}, bf16[128,2048]{1,0:T(8,128)(2,1)S(1)}, u32[]{:S(2)}, u32[]{:S(2)}) %collective-permute-start.21) | collective-permute-done | bytes 524320 | tf_op jit(solution)/shard_map/ppermute | solution.py:23
  213.3 3.0 %collective-permute-start.38 = (bf16[2,128,256]{2,1,0:T(8,128)(2,1)S(1)}, bf16[2,128,256]{2,1,0:T(8,128)(2,1)S(1)}, u32[]{:S(2)}, u32[]{:S(2)}) collective-permute-start(bf16[2,128,256]{2,1,0:T(8,128)(2,1)S(1)} %copy-done.45), channel_id=1, source_target_pairs={{0,96},{16,112},{32,64},{48,80},{64,32},{80,48},{96,0},{112,16},{1... | collective-permute-start | bytes 393224 | tf_op jit(solution)/shard_map/ppermute | solution.py:23
  217.4 6.2 %collective-permute-done.38.refs_20_.refs_22_ = bf16[2,128,256]{2,1,0:T(8,128)(2,1)S(1)} collective-permute-done((bf16[2,128,256]{2,1,0:T(8,128)(2,1)S(1)}, bf16[2,128,256]{2,1,0:T(8,128)(2,1)S(1)}, u32[]{:S(2)}, u32[]{:S(2)}) %collective-permute-start.38) | collective-permute-done | bytes 131104 | tf_op jit(solution)/shard_map/ppermute | solution.py:23
  224.6 4.0 %shard_map.132 = (bf16[128,2048]{1,0:T(8,128)(2,1)}, bf16[128,2048]{1,0:T(8,128)(2,1)}, bf16[128,2048]{1,0:T(8,128)(2,1)}) custom-call(s32[2]{0:T(128)} %pad_add_fusion.seq_ref, bf16[4,128,256]{2,1,0:T(8,128)(2,1)} %get-tuple-element.69.refs_0_.refs_1_.refs_3_.refs_5_, bf16[4,128,256]{2,1,0:T(8,128)(2,1)} %get-tuple-element.69.refs_0_.refs_1_.refs_3_.refs_5_, ...), custom_call_target="tpu_custom_call" | custom-call | tf_op jit(solution)/shard_map/pallas_call | solution.py:53
  (161 shorter events, 61.5 us)
Async XLA Ops:
  8.5 25.7 %collective-permute-start.19 = (bf16[128,2048]{1,0:T(8,128)(2,1)S(1)}, bf16[128,2048]{1,0:T(8,128)(2,1)S(1)}, u32[]{:S(2)}, u32[]{:S(2)}) collective-permute-start(bf16[128,2048]{1,0:T(8,128)(2,1)S(1)} %dynamic-slice_bitcast_fusion), channel_id=1, source_target_pairs={{0,17},{1,16},{2,19},{3,18},{4,21},{5,20},{6,23},{7,22},{8,25},{9,... | collective-permute-start | bytes 1572872 | tf_op jit(solution)/shard_map/ppermute | solution.py:35
  15.0 17.1 %collective-permute-start.7 = (bf16[2,128,512]{2,1,0:T(8,128)(2,1)}, bf16[2,128,512]{2,1,0:T(8,128)(2,1)S(1)}, u32[]{:S(2)}, u32[]{:S(2)}) collective-permute-start(bf16[2,128,512]{2,1,0:T(8,128)(2,1)} %get-tuple-element.55), channel_id=1, source_target_pairs={{0,64},{16,80},{32,96},{48,112},{64,0},{80,16},{96,32},{112,48},{1... | collective-permute-start | bytes 786440 | tf_op jit(solution)/shard_map/ppermute | solution.py:23
  19.4 15.0 %collective-permute-start.13 = (bf16[128,2048]{1,0:T(8,128)(2,1)S(1)}, bf16[128,2048]{1,0:T(8,128)(2,1)S(1)}, u32[]{:S(2)}, u32[]{:S(2)}) collective-permute-start(bf16[128,2048]{1,0:T(8,128)(2,1)S(1)} %dynamic-slice_bitcast_fusion.1), channel_id=1, source_target_pairs={{0,17},{1,16},{2,19},{3,18},{4,21},{5,20},{6,23},{7,22},{8,25},{9,... | collective-permute-start | bytes 1572872 | tf_op jit(solution)/shard_map/ppermute | solution.py:35
  24.0 16.9 %collective-permute-start.24 = (bf16[128,2048]{1,0:T(8,128)(2,1)S(1)}, bf16[128,2048]{1,0:T(8,128)(2,1)S(1)}, u32[]{:S(2)}, u32[]{:S(2)}) collective-permute-start(bf16[128,2048]{1,0:T(8,128)(2,1)S(1)} %bitcast.73), channel_id=1, source_target_pairs={{0,32},{16,48},{32,0},{48,16},{64,96},{80,112},{96,64},{112,80},{1... | collective-permute-start | bytes 1572872 | tf_op jit(solution)/shard_map/ppermute | solution.py:23
  32.1 20.3 %collective-permute-start.25 = (bf16[128,2048]{1,0:T(8,128)(2,1)S(1)}, bf16[128,2048]{1,0:T(8,128)(2,1)S(1)}, u32[]{:S(2)}, u32[]{:S(2)}) collective-permute-start(bf16[128,2048]{1,0:T(8,128)(2,1)S(1)} %bitcast.74), channel_id=1, source_target_pairs={{0,64},{16,80},{32,96},{48,112},{64,0},{80,16},{96,32},{112,48},{1... | collective-permute-start | bytes 1572872 | tf_op jit(solution)/shard_map/ppermute | solution.py:23
  32.5 23.3 %collective-permute-start.26 = (bf16[128,2048]{1,0:T(8,128)(2,1)S(1)}, bf16[128,2048]{1,0:T(8,128)(2,1)S(1)}, u32[]{:S(2)}, u32[]{:S(2)}) collective-permute-start(bf16[128,2048]{1,0:T(8,128)(2,1)S(1)} %bitcast.75), channel_id=1, source_target_pairs={{0,96},{16,112},{32,64},{48,80},{64,32},{80,48},{96,0},{112,16},{1... | collective-permute-start | bytes 1572872 | tf_op jit(solution)/shard_map/ppermute | solution.py:23
  34.2 22.4 %collective-permute-start.20 = (bf16[128,2048]{1,0:T(8,128)(2,1)S(1)}, bf16[128,2048]{1,0:T(8,128)(2,1)S(1)}, u32[]{:S(2)}, u32[]{:S(2)}) collective-permute-start(bf16[128,2048]{1,0:T(8,128)(2,1)S(1)} %collective-permute-done.19.w1), channel_id=1, source_target_pairs={{0,1},{1,0},{2,3},{3,2},{4,5},{5,4},{6,7},{7,6},{8,9},{9,8},{10,11... | collective-permute-start | bytes 1572872 | tf_op jit(solution)/shard_map/ppermute | solution.py:35
  34.4 52.8 %collective-permute-start.14 = (bf16[128,2048]{1,0:T(8,128)(2,1)S(1)}, bf16[128,2048]{1,0:T(8,128)(2,1)S(1)}, u32[]{:S(2)}, u32[]{:S(2)}) collective-permute-start(bf16[128,2048]{1,0:T(8,128)(2,1)S(1)} %collective-permute-done.13.refs_8_.refs_9_.refs_10_.refs_11_.refs_12_.refs_13_.refs_14_.refs_15_.refs_16_.r, ...), channel_id=1, source_target_pairs={{0,1},{1,0},{2,3},{3,2},{4,5},{5,4},{6,7},{7,6},{8,9},{9,8},{10,11... | collective-permute-start | bytes 1572872 | tf_op jit(solution)/shard_map/ppermute | solution.py:35
  40.9 24.9 %collective-permute-start.9 = (bf16[2,128,512]{2,1,0:T(8,128)(2,1)}, bf16[2,128,512]{2,1,0:T(8,128)(2,1)S(1)}, u32[]{:S(2)}, u32[]{:S(2)}) collective-permute-start(bf16[2,128,512]{2,1,0:T(8,128)(2,1)} %get-tuple-element.53.refs_4_), channel_id=1, source_target_pairs={{0,16},{16,0},{32,48},{48,32},{64,80},{80,64},{96,112},{112,96},{1... | collective-permute-start | bytes 786440 | tf_op jit(solution)/shard_map/ppermute | solution.py:23
  52.4 18.9 %collective-permute-start.10 = (bf16[2,128,512]{2,1,0:T(8,128)(2,1)S(1)}, bf16[2,128,512]{2,1,0:T(8,128)(2,1)S(1)}, u32[]{:S(2)}, u32[]{:S(2)}) collective-permute-start(bf16[2,128,512]{2,1,0:T(8,128)(2,1)S(1)} %collective-permute-done.6.refs_5_), channel_id=1, source_target_pairs={{0,16},{16,0},{32,48},{48,32},{64,80},{80,64},{96,112},{112,96},{1... | collective-permute-start | bytes 786440 | tf_op jit(solution)/shard_map/ppermute | solution.py:23
  55.8 18.6 %collective-permute-start.11 = (bf16[2,128,512]{2,1,0:T(8,128)(2,1)S(1)}, bf16[2,128,512]{2,1,0:T(8,128)(2,1)S(1)}, u32[]{:S(2)}, u32[]{:S(2)}) collective-permute-start(bf16[2,128,512]{2,1,0:T(8,128)(2,1)S(1)} %collective-permute-done.7.refs_6_), channel_id=1, source_target_pairs={{0,16},{16,0},{32,48},{48,32},{64,80},{80,64},{96,112},{112,96},{1... | collective-permute-start | bytes 786440 | tf_op jit(solution)/shard_map/ppermute | solution.py:23
  56.6 20.7 %collective-permute-start.12 = (bf16[2,128,512]{2,1,0:T(8,128)(2,1)S(1)}, bf16[2,128,512]{2,1,0:T(8,128)(2,1)S(1)}, u32[]{:S(2)}, u32[]{:S(2)}) collective-permute-start(bf16[2,128,512]{2,1,0:T(8,128)(2,1)S(1)} %collective-permute-done.8.refs_7_), channel_id=1, source_target_pairs={{0,16},{16,0},{32,48},{48,32},{64,80},{80,64},{96,112},{112,96},{1... | collective-permute-start | bytes 786440 | tf_op jit(solution)/shard_map/ppermute | solution.py:23
  65.7 46.7 %collective-permute-start.27 = (bf16[512,512]{1,0:T(8,128)(2,1)}, bf16[512,512]{1,0:T(8,128)(2,1)S(1)}, u32[]{:S(2)}, u32[]{:S(2)}) collective-permute-start(bf16[512,512]{1,0:T(8,128)(2,1)} %shard_map.125), channel_id=1, source_target_pairs={{0,128},{128,0},{1,129},{129,1},{2,130},{130,2},{3,131},{131,3},{4... | collective-permute-start | bytes 1572872 | tf_op jit(solution)/shard_map/ppermute | solution.py:27
  92.5 34.4 %collective-permute-start.15 = (bf16[512,512]{1,0:T(8,128)(2,1)}, bf16[512,512]{1,0:T(8,128)(2,1)S(1)}, u32[]{:S(2)}, u32[]{:S(2)}) collective-permute-start(bf16[512,512]{1,0:T(8,128)(2,1)} %get-tuple-element.58), channel_id=1, source_target_pairs={{0,32},{16,48},{32,0},{48,16},{64,96},{80,112},{96,64},{112,80},{1... | collective-permute-start | bytes 1572872 | tf_op jit(solution)/shard_map/ppermute | solution.py:23
  96.1 14.3 %collective-permute-start = (bf16[1,128,512]{2,1,0:T(8,128)(2,1)}, bf16[1,128,512]{2,1,0:T(8,128)(2,1)S(1)}, u32[]{:S(2)}, u32[]{:S(2)}) collective-permute-start(bf16[1,128,512]{2,1,0:T(8,128)(2,1)} %get-tuple-element.46), channel_id=1, source_target_pairs={{0,32},{16,48},{32,0},{48,16},{64,96},{80,112},{96,64},{112,80},{1... | collective-permute-start | bytes 393224 | tf_op jit(solution)/shard_map/ppermute | solution.py:23
  97.2 33.0 %collective-permute-start.16 = (bf16[512,512]{1,0:T(8,128)(2,1)S(1)}, bf16[512,512]{1,0:T(8,128)(2,1)S(1)}, u32[]{:S(2)}, u32[]{:S(2)}) collective-permute-start(bf16[512,512]{1,0:T(8,128)(2,1)S(1)} %copy-done.44), channel_id=1, source_target_pairs={{0,64},{16,80},{32,96},{48,112},{64,0},{80,16},{96,32},{112,48},{1... | collective-permute-start | bytes 1572872 | tf_op jit(solution)/shard_map/ppermute | solution.py:23
  99.4 30.7 %collective-permute-start.17 = (bf16[512,512]{1,0:T(8,128)(2,1)S(1)}, bf16[512,512]{1,0:T(8,128)(2,1)S(1)}, u32[]{:S(2)}, u32[]{:S(2)}) collective-permute-start(bf16[512,512]{1,0:T(8,128)(2,1)S(1)} %copy-done.43), channel_id=1, source_target_pairs={{0,96},{16,112},{32,64},{48,80},{64,32},{80,48},{96,0},{112,16},{1... | collective-permute-start | bytes 1572872 | tf_op jit(solution)/shard_map/ppermute | solution.py:23
  110.4 15.1 %collective-permute-start.1 = (bf16[1,128,512]{2,1,0:T(8,128)(2,1)}, bf16[1,128,512]{2,1,0:T(8,128)(2,1)S(1)}, u32[]{:S(2)}, u32[]{:S(2)}) collective-permute-start(bf16[1,128,512]{2,1,0:T(8,128)(2,1)} %get-tuple-element.47), channel_id=1, source_target_pairs={{0,64},{16,80},{32,96},{48,112},{64,0},{80,16},{96,32},{112,48},{1... | collective-permute-start | bytes 393224 | tf_op jit(solution)/shard_map/ppermute | solution.py:23
  112.5 14.2 %collective-permute-start.2 = (bf16[1,128,512]{2,1,0:T(8,128)(2,1)}, bf16[1,128,512]{2,1,0:T(8,128)(2,1)S(1)}, u32[]{:S(2)}, u32[]{:S(2)}) collective-permute-start(bf16[1,128,512]{2,1,0:T(8,128)(2,1)} %get-tuple-element.48), channel_id=1, source_target_pairs={{0,96},{16,112},{32,64},{48,80},{64,32},{80,48},{96,0},{112,16},{1... | collective-permute-start | bytes 393224 | tf_op jit(solution)/shard_map/ppermute | solution.py:23
  126.7 17.4 %collective-permute-start.29 = (bf16[512,512]{1,0:T(8,128)(2,1)}, bf16[512,512]{1,0:T(8,128)(2,1)S(1)}, u32[]{:S(2)}, u32[]{:S(2)}) collective-permute-start(bf16[512,512]{1,0:T(8,128)(2,1)} %shard_map.126.refs_0_.refs_1_.refs_12_), channel_id=1, source_target_pairs={{0,64},{16,80},{32,96},{48,112},{64,0},{80,16},{96,32},{112,48},{1... | collective-permute-start | bytes 1572872 | tf_op jit(solution)/shard_map/ppermute | solution.py:23
  126.8 23.1 %collective-permute-start.30 = (bf16[512,512]{1,0:T(8,128)(2,1)}, bf16[512,512]{1,0:T(8,128)(2,1)S(1)}, u32[]{:S(2)}, u32[]{:S(2)}) collective-permute-start(bf16[512,512]{1,0:T(8,128)(2,1)} %shard_map.126.refs_0_.refs_1_.refs_12_), channel_id=1, source_target_pairs={{0,96},{16,112},{32,64},{48,80},{64,32},{80,48},{96,0},{112,16},{1... | collective-permute-start | bytes 1572872 | tf_op jit(solution)/shard_map/ppermute | solution.py:23
  134.8 27.4 %collective-permute-start.18 = (bf16[512,512]{1,0:T(8,128)(2,1)}, bf16[512,512]{1,0:T(8,128)(2,1)S(1)}, u32[]{:S(2)}, u32[]{:S(2)}) collective-permute-start(bf16[512,512]{1,0:T(8,128)(2,1)} %shard_map.123.hid), channel_id=1, source_target_pairs={{0,128},{128,0},{1,129},{129,1},{2,130},{130,2},{3,131},{131,3},{4... | collective-permute-start | bytes 1572872 | tf_op jit(solution)/shard_map/ppermute | solution.py:27
  159.9 29.8 %collective-permute-start.32 = (bf16[2,512,256]{2,1,0:T(8,128)(2,1)}, bf16[2,512,256]{2,1,0:T(8,128)(2,1)S(1)}, u32[]{:S(2)}, u32[]{:S(2)}) collective-permute-start(bf16[2,512,256]{2,1,0:T(8,128)(2,1)} %get-tuple-element.71), channel_id=1, source_target_pairs={{0,16},{16,0},{32,48},{48,32},{64,80},{80,64},{96,112},{112,96},{1... | collective-permute-start | bytes 1572872 | tf_op jit(solution)/shard_map/ppermute | solution.py:23
  169.0 25.5 %collective-permute-start.23 = (bf16[128,2048]{1,0:T(8,128)(2,1)}, bf16[128,2048]{1,0:T(8,128)(2,1)S(1)}, u32[]{:S(2)}, u32[]{:S(2)}) collective-permute-start(bf16[128,2048]{1,0:T(8,128)(2,1)} %get-tuple-element.64), channel_id=1, source_target_pairs={{0,96},{16,112},{32,64},{48,80},{64,32},{80,48},{96,0},{112,16},{1... | collective-permute-start | bytes 1572872 | tf_op jit(solution)/shard_map/ppermute | solution.py:23
  178.5 16.1 %collective-permute-start.31 = (bf16[2,512,256]{2,1,0:T(8,128)(2,1)}, bf16[2,512,256]{2,1,0:T(8,128)(2,1)S(1)}, u32[]{:S(2)}, u32[]{:S(2)}) collective-permute-start(bf16[2,512,256]{2,1,0:T(8,128)(2,1)} %get-tuple-element.66), channel_id=1, source_target_pairs={{0,16},{16,0},{32,48},{48,32},{64,80},{80,64},{96,112},{112,96},{1... | collective-permute-start | bytes 1572872 | tf_op jit(solution)/shard_map/ppermute | solution.py:23
  180.1 22.6 %collective-permute-start.22 = (bf16[128,2048]{1,0:T(8,128)(2,1)S(1)}, bf16[128,2048]{1,0:T(8,128)(2,1)S(1)}, u32[]{:S(2)}, u32[]{:S(2)}) collective-permute-start(bf16[128,2048]{1,0:T(8,128)(2,1)S(1)} %copy-done.42), channel_id=1, source_target_pairs={{0,64},{16,80},{32,96},{48,112},{64,0},{80,16},{96,32},{112,48},{1... | collective-permute-start | bytes 1572872 | tf_op jit(solution)/shard_map/ppermute | solution.py:23
  181.2 26.7 %collective-permute-start.21 = (bf16[128,2048]{1,0:T(8,128)(2,1)S(1)}, bf16[128,2048]{1,0:T(8,128)(2,1)S(1)}, u32[]{:S(2)}, u32[]{:S(2)}) collective-permute-start(bf16[128,2048]{1,0:T(8,128)(2,1)S(1)} %copy-done.41), channel_id=1, source_target_pairs={{0,32},{16,48},{32,0},{48,16},{64,96},{80,112},{96,64},{112,80},{1... | collective-permute-start | bytes 1572872 | tf_op jit(solution)/shard_map/ppermute | solution.py:23
  189.8 38.9 %collective-permute-start.39 = (bf16[256,2048]{1,0:T(8,128)(2,1)}, bf16[256,2048]{1,0:T(8,128)(2,1)S(1)}, u32[]{:S(2)}, u32[]{:S(2)}) collective-permute-start(bf16[256,2048]{1,0:T(8,128)(2,1)} %get-tuple-element.83), channel_id=1, source_target_pairs={{0,16},{16,0},{32,48},{48,32},{64,80},{80,64},{96,112},{112,96},{1... | collective-permute-start | bytes 3145736 | tf_op jit(solution)/shard_map/ppermute | solution.py:23
  194.5 16.2 %collective-permute-start.34 = (bf16[2,128,256]{2,1,0:T(8,128)(2,1)}, bf16[2,128,256]{2,1,0:T(8,128)(2,1)S(1)}, u32[]{:S(2)}, u32[]{:S(2)}) collective-permute-start(bf16[2,128,256]{2,1,0:T(8,128)(2,1)} %get-tuple-element.74), channel_id=1, source_target_pairs={{0,32},{16,48},{32,0},{48,16},{64,96},{80,112},{96,64},{112,80},{1... | collective-permute-start | bytes 393224 | tf_op jit(solution)/shard_map/ppermute | solution.py:23
  194.6 18.7 %collective-permute-start.36 = (bf16[2,128,256]{2,1,0:T(8,128)(2,1)}, bf16[2,128,256]{2,1,0:T(8,128)(2,1)S(1)}, u32[]{:S(2)}, u32[]{:S(2)}) collective-permute-start(bf16[2,128,256]{2,1,0:T(8,128)(2,1)} %get-tuple-element.76), channel_id=1, source_target_pairs={{0,64},{16,80},{32,96},{48,112},{64,0},{80,16},{96,32},{112,48},{1... | collective-permute-start | bytes 393224 | tf_op jit(solution)/shard_map/ppermute | solution.py:23
  202.6 21.0 %collective-permute-start.33 = (bf16[4,128,256]{2,1,0:T(8,128)(2,1)}, bf16[4,128,256]{2,1,0:T(8,128)(2,1)S(1)}, u32[]{:S(2)}, u32[]{:S(2)}) collective-permute-start(bf16[4,128,256]{2,1,0:T(8,128)(2,1)} %get-tuple-element.73), channel_id=1, source_target_pairs={{0,32},{16,48},{32,0},{48,16},{64,96},{80,112},{96,64},{112,80},{1... | collective-permute-start | bytes 786440 | tf_op jit(solution)/shard_map/ppermute | solution.py:23
  207.9 15.7 %collective-permute-start.35 = (bf16[4,128,256]{2,1,0:T(8,128)(2,1)}, bf16[4,128,256]{2,1,0:T(8,128)(2,1)S(1)}, u32[]{:S(2)}, u32[]{:S(2)}) collective-permute-start(bf16[4,128,256]{2,1,0:T(8,128)(2,1)} %get-tuple-element.75), channel_id=1, source_target_pairs={{0,64},{16,80},{32,96},{48,112},{64,0},{80,16},{96,32},{112,48},{1... | collective-permute-start | bytes 786440 | tf_op jit(solution)/shard_map/ppermute | solution.py:23
  (54 other events, 687.9 us)
